TPU v7x, 512 devices: a whole 4x8x8 slice. The times are simulated.
512 devices in a mesh: section: 32 (over x, y), gather: 16 (over z, core).
Axes of the slice: x: 4, y: 8, z: 8, core: 2. Of those that a mesh axis runs over, the one named last changes fastest.
Arguments:
- features: bfloat16 [131072, 512], P(('section', 'gather')), may hold values from -6 to 6
- neighbours: int32 [6, 131072], P(None, ('section', 'gather')), may hold values from 0 to 1279
- send_list: int32 [32, 16, 8, 1], P('section', 'gather'), may hold values from 0 to 1
- cluster: int32 [131072], P(('section', 'gather')), may hold values from 0 to 255, as said below
- coarse_neighbours: int32 [6, 8192], P(None, 'section'), may hold values from 0 to 767
- fine_dst: bfloat16 [512, 512], replicated, may hold values from -0.25 to 0.25
- fine_src: bfloat16 [512, 512], replicated, may hold values from -0.25 to 0.25
- fine_edge: bfloat16 [512, 512], replicated, may hold values from -0.25 to 0.25
- fine_node: bfloat16 [512, 512], replicated, may hold values from -0.25 to 0.25
- fine_bias: float32 [2, 512], replicated, may hold values from -3 to 3
- fine_gain: float32 [512], replicated, may hold values from 0.1 to 1.9
- coarse_dst: bfloat16 [512, 512], replicated, may hold values from -0.25 to 0.25
- coarse_src: bfloat16 [512, 512], replicated, may hold values from -0.25 to 0.25
- coarse_edge: bfloat16 [512, 512], replicated, may hold values from -0.25 to 0.25
- coarse_node: bfloat16 [512, 512], replicated, may hold values from -0.25 to 0.25
- coarse_bias: float32 [2, 512], replicated, may hold values from -3 to 3
- coarse_gain: float32 [512], replicated, may hold values from 0.1 to 1.9
Outputs:
- mesh_out: bfloat16 [131072, 512], P(('section', 'gather'))
Inputs may be any that keep to these rules, and one draw needn't show every extreme that they name: `cluster`: within the 4096 rows of each section group, every coarse node number names exactly 16 rows.
All inputs are finite; a program needn't handle non-finite values.
Results may differ from a plain program's by a relative error of at most 0.0065.
Values may be sent and summed in bfloat16 or wider, within the bound.
No kernel may reach another device: no remote copies, remote signals or barrier semaphores. Data moves between devices by JAX's collectives and lax.ppermute only.
A program may use at most 64 MiB of HBM per device.

v0:
```python
import jax
import jax.numpy as jnp
import numpy as np
from jax import lax
from jax.sharding import PartitionSpec as P

PATCH = 128
POOL = 16


DIRECTIONS = ((-1, -1), (-1, 0), (-1, 1), (0, -1), (0, 1), (1, -1), (1, 0), (1, 1))
EPSILON = 1e-05


def padded(block, sides, width):
    for axis, dim in sides:
        count = lax.axis_size(axis)
        forward = [(i, i + 1) for i in range(count - 1)]
        forward.append((count - 1, 0))
        backward = [(target, source) for source, target in forward]
        low = lax.ppermute(
            lax.slice_in_dim(block, block.shape[dim] - width, None, axis=dim), axis, forward
        )
        high = lax.ppermute(lax.slice_in_dim(block, 0, width, axis=dim), axis, backward)
        block = jnp.concatenate([low, block, high], axis=dim)
    return block


def normalise(values):
    middle = jnp.mean(values, axis=-1, keepdims=True)
    centred = values - middle
    spread = jnp.mean(centred * centred, axis=-1, keepdims=True)
    return centred * lax.rsqrt(spread + EPSILON)


def project(inputs, weight):
    return jnp.dot(inputs, weight, preferred_element_type=jnp.float32).astype(jnp.bfloat16)


def message_update(centre, sources, neighbour_ids, w_target, w_edge, w_node, offsets, gain_row):
    target_term = jnp.dot(centre, w_target, preferred_element_type=jnp.float32) + offsets[0]
    edge_count = neighbour_ids.shape[0]
    picked = jnp.take(sources, neighbour_ids.reshape(-1), axis=0).reshape(
        edge_count, centre.shape[0], sources.shape[1]
    )
    hidden = jax.nn.silu(target_term[None] + picked.astype(jnp.float32)).astype(jnp.bfloat16)
    signals = jax.nn.silu(
        jnp.dot(hidden.reshape(-1, hidden.shape[2]), w_edge, preferred_element_type=jnp.float32)
        + offsets[1]
    )
    summed = jnp.sum(signals.reshape(hidden.shape), axis=0).astype(jnp.bfloat16)
    return gain_row * normalise(jnp.dot(summed, w_node, preferred_element_type=jnp.float32))


def through_halo(pieces, chosen):
    patches = pieces.shape[0]
    beside_all = padded(pieces[None, None], (("section", 0), ("gather", 1)), 1)
    listing = padded(chosen, (("section", 0), ("gather", 1)), 1)
    stacked = beside_all.reshape(9 * patches, pieces.shape[1], pieces.shape[2])
    listing = listing.reshape(9, 8, chosen.shape[3])
    position = np.array(
        [(1 - step_section) * 3 + (1 - step_gather) for step_section, step_gather in DIRECTIONS],
        dtype=np.int32,
    )
    sender_lists = listing[position, np.arange(8)]
    wanted = position[:, None] * patches + sender_lists
    return jnp.take(stacked, wanted.reshape(-1), axis=0)


def coarse_source_rows(outgoing, weight):
    beside_all = padded(outgoing[None], (("section", 0),), 1)
    beside_all = beside_all.reshape(3 * outgoing.shape[0], outgoing.shape[1])
    result_rows = project(beside_all, weight)
    return result_rows


def body(
    features,
    neighbours,
    send_list,
    cluster,
    coarse_neighbours,
    fine_dst,
    fine_src,
    fine_edge,
    fine_node,
    fine_bias,
    fine_gain,
    coarse_dst,
    coarse_src,
    coarse_edge,
    coarse_node,
    coarse_bias,
    coarse_gain,
):
    row_count = features.shape[0]
    feature_width = features.shape[1]
    patches = row_count // PATCH
    slot_count = send_list.shape[3]
    own_sources = project(features, fine_src)
    pieces = features.reshape(patches, PATCH, feature_width)
    arrived = through_halo(pieces, send_list)
    arrived = arrived.reshape(8 * slot_count * PATCH, feature_width)
    ghost_sources = project(arrived, fine_src)
    sources = jnp.concatenate([own_sources, ghost_sources], axis=0)
    update = message_update(
        features, sources, neighbours, fine_dst, fine_edge, fine_node, fine_bias, fine_gain
    )
    fine_rows = (features.astype(jnp.float32) + update).astype(jnp.bfloat16)
    clusters = lax.axis_size("gather") * row_count // POOL
    member = (cluster[None, :] == jnp.arange(clusters, dtype=jnp.int32)[:, None]).astype(
        jnp.bfloat16
    )
    partial_sum = jnp.dot(member, fine_rows, preferred_element_type=jnp.float32)
    totals = lax.psum(partial_sum, "gather")
    pooled = (totals / POOL).astype(jnp.bfloat16)
    coarse_sources = coarse_source_rows(pooled, coarse_src)
    coarse_update = message_update(
        pooled,
        coarse_sources,
        coarse_neighbours,
        coarse_dst,
        coarse_edge,
        coarse_node,
        coarse_bias,
        coarse_gain,
    ).astype(jnp.bfloat16)
    lifted = jnp.take(coarse_update, cluster, axis=0)
    return (fine_rows.astype(jnp.float32) + lifted.astype(jnp.float32)).astype(jnp.bfloat16)


def solution(mesh):
    placed = (
        P(("section", "gather"), None),
        P(None, ("section", "gather")),
        P("section", "gather", None, None),
        P(("section", "gather")),
        P(None, "section"),
        P(),
        P(),
        P(),
        P(),
        P(),
        P(),
        P(),
        P(),
        P(),
        P(),
        P(),
        P(),
    )
    return jax.shard_map(
        body, mesh=mesh, in_specs=placed, out_specs=P(("section", "gather"), None), check_vma=False
    )
```

profile of v0, /device:TPU:1, one launch (start us, length us, event | category | flops | bytes accessed | tf_op | source)
XLA Modules:
  0.0 226.6 jit_solution(12160888750478616806)
XLA Ops:
  6.6 4.2 %collective-permute-start.4 = (bf16[1,1,2,128,512]{4,3,2,1,0:T(8,128)(2,1)}, bf16[1,1,2,128,512]{4,3,2,1,0:T(8,128)(2,1)S(1)}, u32[]{:S(2)}, u32[]{:S(2)}) collective-permute-start(bf16[1,1,2,128,512]{4,3,2,1,0:T(8,128)(2,1)} %bitcast.59), channel_id=1, source_target_pairs={{0,16},{16,32},{32,48},{48,64},{64,80},{80,96},{96,112},{112,128},... | collective-permute-start | bytes 786440 | tf_op jit(solution)/shard_map/ppermute | solution.py:21
  10.8 6.0 %collective-permute-start.5 = (bf16[1,1,2,128,512]{4,3,2,1,0:T(8,128)(2,1)}, bf16[1,1,2,128,512]{4,3,2,1,0:T(8,128)(2,1)S(1)}, u32[]{:S(2)}, u32[]{:S(2)}) collective-permute-start(bf16[1,1,2,128,512]{4,3,2,1,0:T(8,128)(2,1)} %bitcast.60), channel_id=1, source_target_pairs={{16,0},{32,16},{48,32},{64,48},{80,64},{96,80},{112,96},{128,112},... | collective-permute-start | bytes 786440 | tf_op jit(solution)/shard_map/ppermute | solution.py:24
  16.8 1.9 collective-permute-start
  18.7 6.7 %collective-permute-start.1 = (s32[1,1,8,1]{2,3,1,0:T(1,128)}, s32[1,1,8,1]{2,3,1,0:T(1,128)S(1)}, u32[]{:S(2)}, u32[]{:S(2)}) collective-permute-start(s32[1,1,8,1]{2,3,1,0:T(1,128)} %param.24), channel_id=1, source_target_pairs={{16,0},{32,16},{48,32},{64,48},{80,64},{96,80},{112,96},{128,112},... | collective-permute-start | bytes 104 | tf_op jit(solution)/shard_map/ppermute | solution.py:24
  25.4 0.7 compare_select_fusion.4
  26.1 0.7 compare_and_fusion.2
  26.8 2.1 convolution_convert_fusion.2
  28.9 0.7 reshape.153
  29.6 0.7 copy.24
  30.3 0.8 fusion.12
  31.1 0.7 copy.25
  31.9 0.8 fusion.11
  32.6 2.2 convolution_add_fusion.3
  35.0 3.5 %collective-permute-start.6 = (bf16[3,1,2,128,512]{4,3,2,1,0:T(8,128)(2,1)S(1)}, bf16[3,1,2,128,512]{4,3,2,1,0:T(8,128)(2,1)S(1)}, u32[]{:S(2)}, u32[]{:S(2)}) collective-permute-start(bf16[3,1,2,128,512]{4,3,2,1,0:T(8,128)(2,1)S(1)} %pad_maximum_fusion.2), channel_id=1, source_target_pairs={{0,1},{1,2},{2,3},{3,4},{4,5},{5,6},{6,7},{7,8},{8,9},{9,10},{10,1... | collective-permute-start | bytes 2359304 | tf_op jit(solution)/shard_map/ppermute | solution.py:21
  38.5 3.1 %collective-permute-start.7 = (bf16[3,1,2,128,512]{4,3,2,1,0:T(8,128)(2,1)S(1)}, bf16[3,1,2,128,512]{4,3,2,1,0:T(8,128)(2,1)}, u32[]{:S(2)}, u32[]{:S(2)}) collective-permute-start(bf16[3,1,2,128,512]{4,3,2,1,0:T(8,128)(2,1)S(1)} %pad_maximum_fusion.2), channel_id=1, source_target_pairs={{1,0},{2,1},{3,2},{4,3},{5,4},{6,5},{7,6},{8,7},{9,8},{10,9},{11,1... | collective-permute-start | bytes 2359304 | tf_op jit(solution)/shard_map/ppermute | solution.py:24
  41.6 2.9 %collective-permute-start.3 = (s32[3,1,8,1]{2,3,1,0:T(1,128)S(1)}, s32[3,1,8,1]{2,3,1,0:T(1,128)S(1)}, u32[]{:S(2)}, u32[]{:S(2)}) collective-permute-start(s32[3,1,8,1]{2,3,1,0:T(1,128)S(1)} %constant_dynamic-update-slice_fusion), channel_id=1, source_target_pairs={{1,0},{2,1},{3,2},{4,3},{5,4},{6,5},{7,6},{8,7},{9,8},{10,9},{11,1... | collective-permute-start | bytes 296 | tf_op jit(solution)/shard_map/ppermute | solution.py:24
  44.5 2.9 %collective-permute-done.2 = s32[3,1,8,1]{2,3,1,0:T(1,128)S(1)} collective-permute-done((s32[3,1,8,1]{2,3,1,0:T(1,128)S(1)}, s32[3,1,8,1]{2,3,1,0:T(1,128)S(1)}, u32[]{:S(2)}, u32[]{:S(2)}) %collective-permute-start.2) | collective-permute-done | bytes 128 | tf_op jit(solution)/shard_map/ppermute | solution.py:21
  47.5 2.8 %collective-permute-done.3 = s32[3,1,8,1]{2,3,1,0:T(1,128)S(1)} collective-permute-done((s32[3,1,8,1]{2,3,1,0:T(1,128)S(1)}, s32[3,1,8,1]{2,3,1,0:T(1,128)S(1)}, u32[]{:S(2)}, u32[]{:S(2)}) %collective-permute-start.3) | collective-permute-done | bytes 128 | tf_op jit(solution)/shard_map/ppermute | solution.py:24
  50.3 0.6 gather_fusion
  51.1 0.9 copy-done.5
  52.0 1.6 pad_maximum_fusion
  53.6 1.6 gather_fusion.1
  55.2 1.5 bitcast_select_fusion
  56.7 1.7 convolution_convert_fusion
  58.5 5.4 %gather_fusion.2 = bf16[1536,512]{1,0:T(8,128)(2,1)} fusion(bf16[1280,512]{1,0:T(8,128)(2,1)S(1)} %pad_maximum_fusion.1, s32[2048]{0:T(1024)S(1)} %pad_clamp_fusion.1), kind=kCustom, calls=%fused_computation.2 | custom fusion | bytes 3151872 | tf_op jit(solution)/shard_map/jit(_take)/gather | solution.py:43
  63.9 2.4 %multiply_convert_fusion.1 = bf16[1536,512]{1,0:T(8,128)(2,1)S(1)} fusion(bf16[1536,512]{1,0:T(8,128)(2,1)} %gather_fusion.2, f32[256,512]{1,0:T(8,128)S(1)} %copy-done.2, pred[1536]{0:T(1024)(128)(4,1)S(1)} %compare_and_fusion.1), kind=kLoop, calls=%fused_computation.12 | loop fusion | flops 6291456 | bytes 3671552 | tf_op jit(solution)/shard_map/convert_element_type | solution.py:46
  66.3 3.1 %divide_multiply_fusion.1 = f32[1536,512]{1,0:T(8,128)} fusion(bf16[1536,512]{1,0:T(8,128)(2,1)S(1)} %multiply_convert_fusion.1, bf16[512,512]{1,0:T(8,128)(2,1)S(1)} %copy-done, f32[512]{0:T(512)S(1)} %bitcast.74), kind=kOutput, calls=%fused_computation.11 | convolution fusion | flops 809238528 | bytes 5244928 | tf_op jit(solution)/shard_map/dot_general | solution.py:48
  69.4 2.3 %reduce_sum.54 = bf16[256,512]{1,0:T(8,128)(2,1)S(1)} reduce(f32[6,256,512]{2,1,0:T(8,128)} %bitcast.65, f32[]{:T(128)} %constant.82.clone.1), dimensions={0}, to_apply=%region_0.1 | reduce | flops 655360 | bytes 3407876 | tf_op jit(solution)/shard_map/reduce_sum | solution.py:51
  71.8 0.4 fusion.13
  72.2 0.2 multiply_reduce_fusion.1
  72.4 0.2 add_convert_fusion.1
  72.6 1.0 fusion.4
  73.7 115.8 %all-reduce.2.cloned.1.call-done = f32[256,512]{1,0:T(8,128)} async-done(((f32[256,512]{1,0:T(8,128)}), f32[256,512]{1,0:T(8,128)}) %all-reduce.2.cloned.1.call-update) | async-done | bytes 524304 | tf_op jit(solution)/shard_map/psum | solution.py:115
  189.5 1.1 fusion.6
  190.6 3.1 %collective-permute-start.8 = (bf16[1,256,512]{2,1,0:T(8,128)(2,1)S(1)}, bf16[1,256,512]{2,1,0:T(8,128)(2,1)S(1)}, u32[]{:S(2)}, u32[]{:S(2)}) collective-permute-start(bf16[1,256,512]{2,1,0:T(8,128)(2,1)S(1)} %fusion.6), channel_id=1, source_target_pairs={{0,16},{16,32},{32,48},{48,64},{64,80},{80,96},{96,112},{112,128},... | collective-permute-start | bytes 786440 | tf_op jit(solution)/shard_map/ppermute | solution.py:21
  193.7 5.5 %collective-permute-start.9 = (bf16[1,256,512]{2,1,0:T(8,128)(2,1)S(1)}, bf16[1,256,512]{2,1,0:T(8,128)(2,1)S(1)}, u32[]{:S(2)}, u32[]{:S(2)}) collective-permute-start(bf16[1,256,512]{2,1,0:T(8,128)(2,1)S(1)} %fusion.6), channel_id=1, source_target_pairs={{16,0},{32,16},{48,32},{64,48},{80,64},{96,80},{112,96},{128,112},... | collective-permute-start | bytes 786440 | tf_op jit(solution)/shard_map/ppermute | solution.py:24
  199.2 2.1 convolution_add_fusion.2
  201.4 1.6 collective-permute-done.8
  203.0 0.9 collective-permute-done.9
  204.0 0.6 convolution_convert_fusion.1
  204.6 4.8 %gather_fusion.3 = bf16[1536,512]{1,0:T(8,128)(2,1)S(1)} fusion(bf16[768,512]{1,0:T(8,128)(2,1)S(1)} %convolution_convert_fusion.1, s32[2048]{0:T(1024)S(1)} %pad_clamp_fusion), kind=kCustom, calls=%fused_computation.3 | custom fusion | bytes 3151872 | tf_op jit(solution)/shard_map/jit(_take)/gather | solution.py:43
  209.4 2.1 multiply_convert_fusion
  211.5 3.1 %divide_multiply_fusion = f32[1536,512]{1,0:T(8,128)} fusion(bf16[1536,512]{1,0:T(8,128)(2,1)S(1)} %multiply_convert_fusion, bf16[512,512]{1,0:T(8,128)(2,1)S(1)} %copy-done.15, f32[512]{0:T(512)S(1)} %bitcast.73), kind=kOutput, calls=%fused_computation.9 | convolution fusion | flops 809238528 | bytes 5244928 | tf_op jit(solution)/shard_map/dot_general | solution.py:48
  214.6 2.3 %reduce_sum.57 = bf16[256,512]{1,0:T(8,128)(2,1)S(1)} reduce(f32[6,256,512]{2,1,0:T(8,128)} %bitcast.64, f32[]{:T(128)} %constant.82.clone.1), dimensions={0}, to_apply=%region_4.5 | reduce | flops 655360 | bytes 3407876 | tf_op jit(solution)/shard_map/reduce_sum | solution.py:51
  216.9 0.4 fusion.14
  217.3 0.2 multiply_reduce_fusion
  217.7 1.2 gather_fusion.4
  218.9 0.9 add_convert_fusion
  (69 shorter events, 0.8 us)
Async XLA Ops:
  6.5 59.8 %copy-start = (bf16[512,512]{1,0:T(8,128)(2,1)S(1)}, bf16[512,512]{1,0:T(8,128)(2,1)}, u32[]{:S(2)}) copy-start(bf16[512,512]{1,0:T(8,128)(2,1)} %param.29) | copy-start | bytes 1572868
  6.5 43.8 %copy-start.9 = (s32[8]{0:T(128)S(1)}, s32[8]{0:T(128)}, u32[]{:S(2)}) copy-start(s32[8]{0:T(128)} %constant.119) | copy-start | bytes 100
  6.5 44.4 %copy-start.17 = (s32[8]{0:T(128)S(1)}, s32[8]{0:T(128)}, u32[]{:S(2)}) copy-start(s32[8]{0:T(128)} %constant.120) | copy-start | bytes 100
  6.5 28.4 %copy-start.1 = (bf16[256,512]{1,0:T(8,128)(2,1)S(1)}, bf16[256,512]{1,0:T(8,128)(2,1)}, u32[]{:S(2)}) copy-start(bf16[256,512]{1,0:T(8,128)(2,1)} %param.22) | copy-start | bytes 786436
  6.5 28.3 %copy-start.16 = (s32[1,1,8,1]{2,3,1,0:T(1,128)S(1)}, s32[1,1,8,1]{2,3,1,0:T(1,128)}, u32[]{:S(2)}) copy-start(s32[1,1,8,1]{2,3,1,0:T(1,128)} %param.24) | copy-start | bytes 100
  6.5 183.0 %all-reduce.2.cloned.1.call-start = ((), (), s32[]{:S(2)}) async-start(), calls=%async_computation | async-start | bytes 1048576 | tf_op jit(solution)/shard_map/psum | solution.py:115
  6.6 28.3 %collective-permute-start.4 = (bf16[1,1,2,128,512]{4,3,2,1,0:T(8,128)(2,1)}, bf16[1,1,2,128,512]{4,3,2,1,0:T(8,128)(2,1)S(1)}, u32[]{:S(2)}, u32[]{:S(2)}) collective-permute-start(bf16[1,1,2,128,512]{4,3,2,1,0:T(8,128)(2,1)} %bitcast.59), channel_id=1, source_target_pairs={{0,16},{16,32},{32,48},{48,64},{64,80},{80,96},{96,112},{112,128},... | collective-permute-start | bytes 786440 | tf_op jit(solution)/shard_map/ppermute | solution.py:21
  10.8 24.1 %collective-permute-start.5 = (bf16[1,1,2,128,512]{4,3,2,1,0:T(8,128)(2,1)}, bf16[1,1,2,128,512]{4,3,2,1,0:T(8,128)(2,1)S(1)}, u32[]{:S(2)}, u32[]{:S(2)}) collective-permute-start(bf16[1,1,2,128,512]{4,3,2,1,0:T(8,128)(2,1)} %bitcast.60), channel_id=1, source_target_pairs={{16,0},{32,16},{48,32},{64,48},{80,64},{96,80},{112,96},{128,112},... | collective-permute-start | bytes 786440 | tf_op jit(solution)/shard_map/ppermute | solution.py:24
  16.8 18.1 %collective-permute-start = (s32[1,1,8,1]{2,3,1,0:T(1,128)}, s32[1,1,8,1]{2,3,1,0:T(1,128)S(1)}, u32[]{:S(2)}, u32[]{:S(2)}) collective-permute-start(s32[1,1,8,1]{2,3,1,0:T(1,128)} %param.24), channel_id=1, source_target_pairs={{0,16},{16,32},{32,48},{48,64},{64,80},{80,96},{96,112},{112,128},... | collective-permute-start | bytes 104 | tf_op jit(solution)/shard_map/ppermute | solution.py:21
  18.7 22.9 %collective-permute-start.1 = (s32[1,1,8,1]{2,3,1,0:T(1,128)}, s32[1,1,8,1]{2,3,1,0:T(1,128)S(1)}, u32[]{:S(2)}, u32[]{:S(2)}) collective-permute-start(s32[1,1,8,1]{2,3,1,0:T(1,128)} %param.24), channel_id=1, source_target_pairs={{16,0},{32,16},{48,32},{64,48},{80,64},{96,80},{112,96},{128,112},... | collective-permute-start | bytes 104 | tf_op jit(solution)/shard_map/ppermute | solution.py:24
  34.9 15.3 %copy-start.4 = (bf16[1,1,2,128,512]{4,3,2,1,0:T(8,128)(2,1)}, bf16[1,1,2,128,512]{4,3,2,1,0:T(8,128)(2,1)S(1)}, u32[]{:S(2)}) copy-start(bf16[1,1,2,128,512]{4,3,2,1,0:T(8,128)(2,1)S(1)} %collective-permute-done.5) | copy-start | bytes 786436
  35.0 16.0 %collective-permute-start.6 = (bf16[3,1,2,128,512]{4,3,2,1,0:T(8,128)(2,1)S(1)}, bf16[3,1,2,128,512]{4,3,2,1,0:T(8,128)(2,1)S(1)}, u32[]{:S(2)}, u32[]{:S(2)}) collective-permute-start(bf16[3,1,2,128,512]{4,3,2,1,0:T(8,128)(2,1)S(1)} %pad_maximum_fusion.2), channel_id=1, source_target_pairs={{0,1},{1,2},{2,3},{3,4},{4,5},{5,6},{6,7},{7,8},{8,9},{9,10},{10,1... | collective-permute-start | bytes 2359304 | tf_op jit(solution)/shard_map/ppermute | solution.py:21
  38.5 13.4 %collective-permute-start.7 = (bf16[3,1,2,128,512]{4,3,2,1,0:T(8,128)(2,1)S(1)}, bf16[3,1,2,128,512]{4,3,2,1,0:T(8,128)(2,1)}, u32[]{:S(2)}, u32[]{:S(2)}) collective-permute-start(bf16[3,1,2,128,512]{4,3,2,1,0:T(8,128)(2,1)S(1)} %pad_maximum_fusion.2), channel_id=1, source_target_pairs={{1,0},{2,1},{3,2},{4,3},{5,4},{6,5},{7,6},{8,7},{9,8},{10,9},{11,1... | collective-permute-start | bytes 2359304 | tf_op jit(solution)/shard_map/ppermute | solution.py:24
  41.6 5.9 %collective-permute-start.2 = (s32[3,1,8,1]{2,3,1,0:T(1,128)S(1)}, s32[3,1,8,1]{2,3,1,0:T(1,128)S(1)}, u32[]{:S(2)}, u32[]{:S(2)}) collective-permute-start(s32[3,1,8,1]{2,3,1,0:T(1,128)S(1)} %constant_dynamic-update-slice_fusion), channel_id=1, source_target_pairs={{0,1},{1,2},{2,3},{3,4},{4,5},{5,6},{6,7},{7,8},{8,9},{9,10},{10,1... | collective-permute-start | bytes 296 | tf_op jit(solution)/shard_map/ppermute | solution.py:21
  41.6 8.6 %collective-permute-start.3 = (s32[3,1,8,1]{2,3,1,0:T(1,128)S(1)}, s32[3,1,8,1]{2,3,1,0:T(1,128)S(1)}, u32[]{:S(2)}, u32[]{:S(2)}) collective-permute-start(s32[3,1,8,1]{2,3,1,0:T(1,128)S(1)} %constant_dynamic-update-slice_fusion), channel_id=1, source_target_pairs={{1,0},{2,1},{3,2},{4,3},{5,4},{6,5},{7,6},{8,7},{9,8},{10,9},{11,1... | collective-permute-start | bytes 296 | tf_op jit(solution)/shard_map/ppermute | solution.py:24
  51.1 0.9 copy-start.5
  55.2 3.2 %copy-start.3 = (bf16[256,512]{1,0:T(8,128)(2,1)S(1)}, bf16[256,512]{1,0:T(8,128)(2,1)}, u32[]{:S(2)}) copy-start(bf16[256,512]{1,0:T(8,128)(2,1)} %convolution_convert_fusion.2) | copy-start | bytes 786436
  58.5 5.4 %copy-start.2 = (f32[256,512]{1,0:T(8,128)S(1)}, f32[256,512]{1,0:T(8,128)}, u32[]{:S(2)}) copy-start(f32[256,512]{1,0:T(8,128)} %convolution_add_fusion.3) | copy-start | bytes 1572868
  69.4 2.3 %copy-start.6 = (bf16[512,512]{1,0:T(8,128)(2,1)S(1)}, bf16[512,512]{1,0:T(8,128)(2,1)}, u32[]{:S(2)}) copy-start(bf16[512,512]{1,0:T(8,128)(2,1)} %param.30) | copy-start | bytes 1572868
  69.4 3.0 %copy-start.12 = (f32[512]{0:T(512)S(1)}, f32[512]{0:T(512)}, u32[]{:S(2)}) copy-start(f32[512]{0:T(512)} %param.32) | copy-start | bytes 6148
  69.4 3.2 %copy-start.11 = (s32[256]{0:T(256)S(1)}, s32[256]{0:T(256)}, u32[]{:S(2)}) copy-start(s32[256]{0:T(256)} %param.25) | copy-start | bytes 3076
  71.8 1.9 copy-start.10
  71.8 127.5 %copy-start.7 = (bf16[512,512]{1,0:T(8,128)(2,1)S(1)}, bf16[512,512]{1,0:T(8,128)(2,1)}, u32[]{:S(2)}) copy-start(bf16[512,512]{1,0:T(8,128)(2,1)} %param.33) | copy-start | bytes 1572868
  73.6 130.4 %copy-start.14 = (bf16[512,512]{1,0:T(8,128)(2,1)S(1)}, bf16[512,512]{1,0:T(8,128)(2,1)}, u32[]{:S(2)}) copy-start(bf16[512,512]{1,0:T(8,128)(2,1)} %param.34) | copy-start | bytes 1572868
  190.6 12.4 %collective-permute-start.8 = (bf16[1,256,512]{2,1,0:T(8,128)(2,1)S(1)}, bf16[1,256,512]{2,1,0:T(8,128)(2,1)S(1)}, u32[]{:S(2)}, u32[]{:S(2)}) collective-permute-start(bf16[1,256,512]{2,1,0:T(8,128)(2,1)S(1)} %fusion.6), channel_id=1, source_target_pairs={{0,16},{16,32},{32,48},{48,64},{64,80},{80,96},{96,112},{112,128},... | collective-permute-start | bytes 786440 | tf_op jit(solution)/shard_map/ppermute | solution.py:21
  193.7 10.2 %collective-permute-start.9 = (bf16[1,256,512]{2,1,0:T(8,128)(2,1)S(1)}, bf16[1,256,512]{2,1,0:T(8,128)(2,1)S(1)}, u32[]{:S(2)}, u32[]{:S(2)}) collective-permute-start(bf16[1,256,512]{2,1,0:T(8,128)(2,1)S(1)} %fusion.6), channel_id=1, source_target_pairs={{16,0},{32,16},{48,32},{64,48},{80,64},{96,80},{112,96},{128,112},... | collective-permute-start | bytes 786440 | tf_op jit(solution)/shard_map/ppermute | solution.py:24
  209.4 2.1 copy-start.15
  214.6 2.3 %copy-start.8 = (bf16[512,512]{1,0:T(8,128)(2,1)S(1)}, bf16[512,512]{1,0:T(8,128)(2,1)}, u32[]{:S(2)}) copy-start(bf16[512,512]{1,0:T(8,128)(2,1)} %param.36) | copy-start | bytes 1572868
  214.6 3.0 %copy-start.13 = (f32[512]{0:T(512)S(1)}, f32[512]{0:T(512)}, u32[]{:S(2)}) copy-start(f32[512]{0:T(512)} %param.38) | copy-start | bytes 6148
Sparse Core Ops, SparseCore 0:
  73.8 115.7 all-reduce.1
where the time goes:
time: 228 us; the launch traced here: 227 us
  waiting for transfers between devices  124 us (54%)
  starting transfers between devices  36.9 us (16%)
  local copies, waits for them, and re-layouts  18.3 us (8%)
  matrix products  16.8 us (7%)
  other arithmetic  16.6 us (7%)
  between operations  13.8 us (6%)
    psum x1, waiting for transfers between devices, body(): totals = lax.psum(partial_sum, 'gather')  116 us
    ppermute x5, starting transfers between devices, padded(): lax.ppermute(lax.slice_in_dim(block, 0, width, axis=dim), axis, backward)  24.2 us
    ppermute x5, starting transfers between devices, padded(): lax.ppermute(lax.slice_in_dim(block, block.shape[dim] - width, None, axis...  12.7 us
    gather x2, local copies, waits for them, and re-layouts, message_update(): jnp.take(sources, neighbour_ids.reshape(-1), axis=0)  10.2 us
    dot_general x2, matrix products, message_update(): jnp.dot(hidden.reshape(-1, hidden.shape[2]), w_edge, preferred_element_ty...  6.16 us
    reduce_sum x2, other arithmetic, message_update(): summed = jnp.sum(signals.reshape(hidden.shape), axis=0).astype(jnp.bfloat16)  4.65 us
    ppermute x5, waiting for transfers between devices, padded(): lax.ppermute(lax.slice_in_dim(block, block.shape[dim] - width, None, axis...  4.56 us
  transfers between devices with their start and end apart: 11, of which 5 were waited for; matrix products, arithmetic and copies ran while one was open for 6% of the time, Pallas kernels for 0%

commit v1 on v0

v1 whole, which is shorter than its diff:
```python
import jax
import jax.numpy as jnp
from jax import lax
from jax.experimental import pallas as pl
from jax.experimental.pallas import tpu as pltpu
from jax.sharding import PartitionSpec as P

PATCH = 128
POOL = 16
META = 16
EPSILON = 1e-05
F32 = jnp.float32
BF16 = jnp.bfloat16


def shifted(block, axis, step):
    count = lax.axis_size(axis)
    return lax.ppermute(block, axis, [(i, (i + step) % count) for i in range(count)])


def dot(left, right):
    return jnp.dot(left, right, preferred_element_type=F32)


def one_hot(column, width, value):
    lanes = lax.broadcasted_iota(jnp.int32, (column.shape[0], width), 1)
    return jnp.where(column == lanes, F32(value), F32(0)).astype(BF16)


def silu_of_half(half):
    return half * jnp.tanh(half) + half


def normalise(values):
    middle = jnp.mean(values, axis=-1, keepdims=True)
    centred = values - middle
    spread = jnp.mean(centred * centred, axis=-1, keepdims=True)
    return centred * lax.rsqrt(spread + EPSILON)


def messages(ids, sources, target_half, edge, node, bias_half, gain):
    half_edge = edge * BF16(0.5)
    total = None
    for e in range(6):
        chosen = one_hot(ids[:, e : e + 1], sources.shape[0], 0.5)
        hidden = silu_of_half(dot(chosen, sources) + target_half).astype(BF16)
        signal = silu_of_half(dot(hidden, half_edge) + bias_half)
        total = signal if total is None else total + signal
    return gain * normalise(dot(total.astype(BF16), node))


def fine_kernel(
    features, own_sources, target_half, beside, below, above, ids, cluster, src, edge, node, bias, gain,
    rows_out, partial_out, sources,
):
    rows = features.shape[0]

    def place(number, value):
        sources[pl.ds(rows + PATCH * number, PATCH), :] = value

    sources[pl.ds(0, rows), :] = own_sources[...]
    near = dot(beside[...], src[...]).astype(BF16)
    place(1, near[:PATCH])
    place(6, near[PATCH:])
    for piece, numbers in ((above, (0, 3, 5)), (below, (2, 4, 7))):
        projected = dot(piece[...], src[...]).astype(BF16)
        for k, number in enumerate(numbers):
            place(number, projected[k * PATCH : (k + 1) * PATCH])
    update = messages(
        ids[...], sources[...], target_half[...], edge[...], node[...], 0.5 * bias[1:2, :], gain[...]
    )
    fine_rows = (features[...].astype(F32) + update).astype(BF16)
    rows_out[...] = fine_rows
    clusters = partial_out.shape[0]
    member = lax.broadcasted_iota(jnp.int32, (clusters, rows), 0) == cluster[...]
    member = jnp.where(member, F32(1), F32(0)).astype(BF16)
    partial_out[...] = dot(member, fine_rows).astype(BF16)


def coarse_kernel(spread, fine_rows, ids, cluster, dst, src, edge, node, bias, gain, out, pooled):
    shares = spread.shape[0] // 48
    for k in range(shares):
        pooled[pl.ds(16 * k, 16), :] = spread[pl.ds(48 * k + 16, 16), :]
    clusters = pooled.shape[0]
    sources = dot(spread[...], src[...]).astype(BF16)
    target_half = 0.5 * (dot(pooled[...], dst[...]) + bias[0:1, :])
    place = ids[...]
    within = place & (clusters - 1)
    place = (within >> 4) * 48 + (place >> 8) * 16 + (within & 15)
    update = messages(
        place, sources, target_half, edge[...], node[...], 0.5 * bias[1:2, :], gain[...]
    ).astype(BF16)
    lifted = dot(one_hot(cluster[...], clusters, 1.0), update)
    out[...] = (fine_rows[...].astype(F32) + lifted).astype(BF16)


def body(
    features,
    neighbours,
    send_list,
    cluster,
    coarse_neighbours,
    fine_dst,
    fine_src,
    fine_edge,
    fine_node,
    fine_bias,
    fine_gain,
    coarse_dst,
    coarse_src,
    coarse_edge,
    coarse_node,
    coarse_bias,
    coarse_gain,
):
    rows, width = features.shape
    shares = lax.axis_size("gather")
    clusters = shares * rows // POOL
    share = clusters // shares
    listing = jnp.broadcast_to(send_list.reshape(8, 1).astype(BF16), (8, width))
    own = jnp.concatenate([features, listing, jnp.zeros((META - 8, width), BF16)], axis=0)
    before = shifted(own, "section", 1)
    after = shifted(own, "section", -1)

    def chosen(block, number):
        return jnp.where(block[rows + number][None, :] > 0.5, block[PATCH:rows], block[:PATCH])

    own_sources = dot(features, fine_src).astype(BF16)
    target_half = 0.5 * (dot(features, fine_dst) + fine_bias[0])
    ids = jnp.pad(neighbours.T, ((0, 0), (0, 2)))
    coarse_ids = jnp.pad(coarse_neighbours.T, ((0, 0), (0, 2)))
    to_next = jnp.concatenate([chosen(after, 2), chosen(own, 4), chosen(before, 7)], axis=0)
    to_last = jnp.concatenate([chosen(after, 0), chosen(own, 3), chosen(before, 5)], axis=0)
    below = shifted(to_next, "gather", 1)
    above = shifted(to_last, "gather", -1)
    beside = jnp.concatenate([chosen(after, 1), chosen(before, 6)], axis=0)

    fine_rows, partial = pl.pallas_call(
        fine_kernel,
        out_shape=(
            jax.ShapeDtypeStruct((rows, width), BF16),
            jax.ShapeDtypeStruct((clusters, width), BF16),
        ),
        scratch_shapes=[pltpu.VMEM((rows + 8 * PATCH, width), BF16)],
        name="fine",
    )(
        features, own_sources, target_half, beside, below, above, ids, cluster[None, :],
        fine_src, fine_edge, fine_node, fine_bias, fine_gain[None, :],
    )

    parts = lax.all_to_all(partial.reshape(shares, share, width), "gather", 0, 0, tiled=True)
    pooled = (jnp.sum(parts.astype(F32), axis=0) / POOL).astype(BF16)
    sides = [shifted(pooled, "section", 1), pooled, shifted(pooled, "section", -1)]
    spread = lax.all_gather(jnp.concatenate(sides, axis=0), "gather", axis=0, tiled=True)

    return pl.pallas_call(
        coarse_kernel,
        out_shape=jax.ShapeDtypeStruct((rows, width), BF16),
        scratch_shapes=[pltpu.VMEM((clusters, width), BF16)],
        name="coarse",
    )(
        spread, fine_rows, coarse_ids, cluster[:, None],
        coarse_dst, coarse_src, coarse_edge, coarse_node, coarse_bias, coarse_gain[None, :],
    )


def solution(mesh):
    placed = (
        P(("section", "gather"), None),
        P(None, ("section", "gather")),
        P("section", "gather", None, None),
        P(("section", "gather")),
        P(None, "section"),
    ) + (P(),) * 12
    return jax.shard_map(
        body, mesh=mesh, in_specs=placed, out_specs=P(("section", "gather"), None), check_vma=False
    )
```

time: 228 us -> 100 us (0.44)
  waiting for transfers between devices: 124 us -> 11.5 us
  blocking collectives: 0 us -> 40.2 us
  matrix products: 16.8 us -> 2.09 us
  Pallas kernels: 0 us -> 14.5 us
  starting transfers between devices: 36.9 us -> 22.5 us
  local copies, waits for them, and re-layouts: 18.3 us -> 4.54 us
  other arithmetic: 16.6 us -> 2.87 us
  between operations: 13.8 us -> 1.44 us
    psum x1 -> x0, waiting for transfers between devices: 116 us -> none  [body(): totals = lax.psum(partial_sum, 'gather')]
    all_to_all x0 -> x1, blocking collectives: none -> 22.2 us  [body(): lax.all_to_all(partial.reshape(shares, share, width), 'gather', 0, 0, til...]
    all_gather x0 -> x1, blocking collectives: none -> 18 us  [body(): lax.all_gather(jnp.concatenate(sides, axis=0), 'gather', axis=0, tiled=True)]
    dot_general x10 -> x2, matrix products: 16.8 us -> 2.09 us  [dot(): return jnp.dot(left, right, preferred_element_type=F32)]
    pallas_call x0 -> x2, Pallas kernels: none -> 14.5 us  [the longest x1 7.73 us: body(): pl.pallas_call(fine_kernel, out_shape=(jax.ShapeDtypeStruct((rows, width)...]
    ppermute x10 -> x6, starting transfers between devices: 36.9 us -> 22.5 us  [shifted(): lax.ppermute(block, axis, [(i, (i + step) % count) for i in range(count)])]
    gather x5 -> x0, local copies, waits for them, and re-layouts: 13.6 us -> none  [the longest x2 10.2 us: message_update(): jnp.take(sources, neighbour_ids.reshape(-1), axis=0)]
    reduce_sum x4 -> x1, other arithmetic: 5.07 us -> 0.04 us  [body(): pooled = (jnp.sum(parts.astype(F32), axis=0) / POOL).astype(BF16)]
  transfers between devices with their start and end apart: 11 -> 6, of which waited for: 5 -> 4; matrix products, arithmetic and copies ran while one was open for 6% -> 6% of each run, Pallas kernels for 0% -> 0%
where the time goes in v1:
time: 100 us; the launch traced here: 99.7 us
  blocking collectives  40.2 us (40%)
  starting transfers between devices  22.5 us (22%)
  Pallas kernels  14.5 us (14%)
  waiting for transfers between devices  11.5 us (12%)
  local copies, waits for them, and re-layouts  4.54 us (5%)
  other arithmetic  2.87 us (3%)
  matrix products  2.09 us (2%)
  between operations  1.44 us (1%)
    ppermute x6, starting transfers between devices, shifted(): lax.ppermute(block, axis, [(i, (i + step) % count) for i in range(count)])  22.5 us
    all_to_all x1, blocking collectives, body(): lax.all_to_all(partial.reshape(shares, share, width), 'gather', 0, 0, til...  22.2 us
    all_gather x1, blocking collectives, body(): lax.all_gather(jnp.concatenate(sides, axis=0), 'gather', axis=0, tiled=True)  18 us
    ppermute x6, waiting for transfers between devices, shifted(): lax.ppermute(block, axis, [(i, (i + step) % count) for i in range(count)])  11.5 us
    pallas_call x1, Pallas kernels, body(): pl.pallas_call(fine_kernel, out_shape=(jax.ShapeDtypeStruct((rows, width)...  7.73 us
    pallas_call x1, Pallas kernels, body(): pl.pallas_call(coarse_kernel, out_shape=jax.ShapeDtypeStruct((rows, width...  6.8 us
    dot_general x2, matrix products, dot(): return jnp.dot(left, right, preferred_element_type=F32)  2.09 us
  transfers between devices with their start and end apart: 6, of which 4 were waited for; matrix products, arithmetic and copies ran while one was open for 6% of the time, Pallas kernels for 0%

profile of v1, /device:TPU:1, one launch (start us, length us, event | category | flops | bytes accessed | tf_op | source)
XLA Modules:
  0.0 99.7 jit_solution(15382371820825843310)
XLA Ops:
  0.0 0.0 copy-start
  0.0 0.7 fusion.2
  0.7 0.1 pad.22.clone
  0.8 0.0 copy-start.1
  0.8 1.2 %maximum_maximum_fusion = bf16[272,512]{1,0:T(8,128)(2,1)S(1)} fusion(bf16[256,512]{1,0:T(8,128)(2,1)} %features.1, bf16[272]{0:T(512)(128)(2,1)S(1)} %pad.22.clone, bf16[272]{0:T(512)(128)(2,1)S(1)} %pad.21.clone), kind=kLoop, calls=%fused_computation.6 | loop fusion | flops 835584 | bytes 541760 | tf_op jit(solution)/shard_map/concatenate | solution.py:121
  2.0 8.1 %collective-permute-start = (bf16[272,512]{1,0:T(8,128)(2,1)S(1)}, bf16[272,512]{1,0:T(8,128)(2,1)S(1)}, u32[]{:S(2)}, u32[]{:S(2)}) collective-permute-start(bf16[272,512]{1,0:T(8,128)(2,1)S(1)} %maximum_maximum_fusion), channel_id=1, source_target_pairs={{0,496},{16,0},{32,16},{48,32},{64,48},{80,64},{96,80},{112,96},{1... | collective-permute-start | bytes 835592 | tf_op jit(solution)/shard_map/ppermute | solution.py:18
  10.1 1.9 %collective-permute-start.1 = (bf16[272,512]{1,0:T(8,128)(2,1)S(1)}, bf16[272,512]{1,0:T(8,128)(2,1)S(1)}, u32[]{:S(2)}, u32[]{:S(2)}) collective-permute-start(bf16[272,512]{1,0:T(8,128)(2,1)S(1)} %maximum_maximum_fusion), channel_id=1, source_target_pairs={{0,16},{16,32},{32,48},{48,64},{64,80},{80,96},{96,112},{112,128},... | collective-permute-start | bytes 835592 | tf_op jit(solution)/shard_map/ppermute | solution.py:18
  12.0 0.6 fusion.1
  13.9 0.0 copy-done.1
  13.9 1.5 %collective-permute-done = bf16[272,512]{1,0:T(8,128)(2,1)S(1)} collective-permute-done((bf16[272,512]{1,0:T(8,128)(2,1)S(1)}, bf16[272,512]{1,0:T(8,128)(2,1)S(1)}, u32[]{:S(2)}, u32[]{:S(2)}) %collective-permute-start) | collective-permute-done | bytes 278560 | tf_op jit(solution)/shard_map/ppermute | solution.py:18
  15.5 7.1 %collective-permute-done.1 = bf16[272,512]{1,0:T(8,128)(2,1)S(1)} collective-permute-done((bf16[272,512]{1,0:T(8,128)(2,1)S(1)}, bf16[272,512]{1,0:T(8,128)(2,1)S(1)}, u32[]{:S(2)}, u32[]{:S(2)}) %collective-permute-start.1) | collective-permute-done | bytes 278560 | tf_op jit(solution)/shard_map/ppermute | solution.py:18
  22.7 0.0 copy-start.2
  22.7 1.8 %collective-permute-start.3 = (bf16[384,512]{1,0:T(8,128)(2,1)S(1)}, bf16[384,512]{1,0:T(8,128)(2,1)S(1)}, u32[]{:S(2)}, u32[]{:S(2)}) collective-permute-start(bf16[384,512]{1,0:T(8,128)(2,1)S(1)} %pad_maximum_fusion.1), channel_id=1, source_target_pairs={{0,15},{1,0},{2,1},{3,2},{4,3},{5,4},{6,5},{7,6},{8,7},{9,8},{10,9... | collective-permute-start | bytes 1179656 | tf_op jit(solution)/shard_map/ppermute | solution.py:18
  24.6 2.0 %collective-permute-start.2 = (bf16[384,512]{1,0:T(8,128)(2,1)S(1)}, bf16[384,512]{1,0:T(8,128)(2,1)S(1)}, u32[]{:S(2)}, u32[]{:S(2)}) collective-permute-start(bf16[384,512]{1,0:T(8,128)(2,1)S(1)} %pad_maximum_fusion), channel_id=1, source_target_pairs={{0,1},{1,2},{2,3},{3,4},{4,5},{5,6},{6,7},{7,8},{8,9},{9,10},{10,1... | collective-permute-start | bytes 1179656 | tf_op jit(solution)/shard_map/ppermute | solution.py:18
  26.6 0.0 copy-done.2
  26.6 0.0 copy-start.5
  26.6 1.0 %convolution_convert_fusion.own_sources = bf16[256,512]{1,0:T(8,128)(2,1)} fusion(bf16[256,512]{1,0:T(8,128)(2,1)S(1)} %copy-done.1, bf16[512,512]{1,0:T(8,128)(2,1)S(1)} %copy-done.2), kind=kOutput, calls=%fused_computation.2 | convolution fusion | flops 134348800 | bytes 1048576 | tf_op jit(solution)/shard_map/dot_general | solution.py:22
  27.6 0.0 copy-done.5
  27.6 0.1 copy.20
  27.8 0.0 slice-start
  27.8 0.7 pad.7.ids
  28.4 0.0 copy-done
  28.4 0.0 slice-done
  28.4 1.1 %fusion.target_half = f32[256,512]{1,0:T(8,128)} fusion(bf16[256,512]{1,0:T(8,128)(2,1)S(1)} %copy-done.1, bf16[512,512]{1,0:T(8,128)(2,1)S(1)} %copy-done, f32[512]{0:T(512)S(1)} %bitcast.19), kind=kOutput, calls=%fused_computation.1 | convolution fusion | flops 134479872 | bytes 1312768 | tf_op jit(solution)/shard_map/dot_general | solution.py:22
  29.5 0.7 pad_maximum_fusion.2.beside
  30.3 1.7 %collective-permute-done.3.above = bf16[384,512]{1,0:T(8,128)(2,1)S(1)} collective-permute-done((bf16[384,512]{1,0:T(8,128)(2,1)S(1)}, bf16[384,512]{1,0:T(8,128)(2,1)S(1)}, u32[]{:S(2)}, u32[]{:S(2)}) %collective-permute-start.3) | collective-permute-done | bytes 393248 | tf_op jit(solution)/shard_map/ppermute | solution.py:18
  32.0 0.0 copy-start.3
  32.0 1.2 %collective-permute-done.2.below = bf16[384,512]{1,0:T(8,128)(2,1)S(1)} collective-permute-done((bf16[384,512]{1,0:T(8,128)(2,1)S(1)}, bf16[384,512]{1,0:T(8,128)(2,1)S(1)}, u32[]{:S(2)}, u32[]{:S(2)}) %collective-permute-start.2) | collective-permute-done | bytes 393248 | tf_op jit(solution)/shard_map/ppermute | solution.py:18
  33.2 0.0 copy-start.4
  33.2 0.0 copy-done.3
  33.2 0.7 copy-done.4
  33.9 7.7 %fine.1 = (bf16[256,512]{1,0:T(8,128)(2,1)}, bf16[256,512]{1,0:T(8,128)(2,1)}) custom-call(bf16[256,512]{1,0:T(8,128)(2,1)} %features.1, bf16[256,512]{1,0:T(8,128)(2,1)} %convolution_convert_fusion.own_sources, f32[256,512]{1,0:T(8,128)} %fusion.target_half, bf16[256,512]{1,0:T(8,128)(2,1)} %pad_maximum_fusion.2.beside, bf16[384,512]{1,0:T(8,128)(2,1)} %copy-done.4, ...), custom_call_target="tpu_custom_call" | custom-call | tf_op jit(solution)/shard_map/fine/pallas_call | solution.py:138
  41.7 22.2 %all_to_all.5 = bf16[16,16,512]{2,1,0:T(8,128)(2,1)S(1)} all-to-all(bf16[16,16,512]{2,1,0:T(8,128)(2,1)} %bitcast.18), channel_id=1, replica_groups=mesh['section'=32,'gather'=16] {'gather'}, dimensions={0} | all-to-all | bytes 524288 | tf_op jit(solution)/shard_map/all_to_all | solution.py:151
  63.9 0.0 copy-start.6
  63.9 1.9 %collective-permute-start.4 = (bf16[16,512]{1,0:T(8,128)(2,1)S(1)}, bf16[16,512]{1,0:T(8,128)(2,1)S(1)}, u32[]{:S(2)}, u32[]{:S(2)}) collective-permute-start(bf16[16,512]{1,0:T(8,128)(2,1)S(1)} %multiply_convert_fusion), channel_id=1, source_target_pairs={{0,16},{16,32},{32,48},{48,64},{64,80},{80,96},{96,112},{112,128},... | collective-permute-start | bytes 49160 | tf_op jit(solution)/shard_map/ppermute | solution.py:18
  65.9 6.7 %collective-permute-start.5 = (bf16[16,512]{1,0:T(8,128)(2,1)S(1)}, bf16[16,512]{1,0:T(8,128)(2,1)S(1)}, u32[]{:S(2)}, u32[]{:S(2)}) collective-permute-start(bf16[16,512]{1,0:T(8,128)(2,1)S(1)} %multiply_convert_fusion), channel_id=1, source_target_pairs={{0,496},{16,0},{32,16},{48,32},{64,48},{80,64},{96,80},{112,96},{1... | collective-permute-start | bytes 49160 | tf_op jit(solution)/shard_map/ppermute | solution.py:18
  72.6 0.0 copy-done.6
  72.6 0.1 copy.21
  72.7 0.7 pad.8.ids
  73.4 0.0 copy-start.7
  73.4 0.7 copy-done.7
  74.0 0.8 copy.22.cluster
  74.8 0.0 collective-permute-done.4
  74.8 0.0 collective-permute-done.5
  74.9 18.0 %all_gather.3.spread = bf16[768,512]{1,0:T(8,128)(2,1)} all-gather(bf16[48,512]{1,0:T(8,128)(2,1)S(1)} %pad_maximum_fusion.3), channel_id=1, replica_groups=mesh['section'=32,'gather'=16] {'gather'}, dimensions={0}, use_global_device_ids=true | all-gather | bytes 835584 | tf_op jit(solution)/shard_map/all_gather | solution.py:154
  92.9 6.8 %coarse.1 = bf16[256,512]{1,0:T(8,128)(2,1)} custom-call(bf16[768,512]{1,0:T(8,128)(2,1)} %all_gather.3.spread, bf16[256,512]{1,0:T(8,128)(2,1)} %get-tuple-element.8.fine_rows, s32[256,8]{1,0:T(8,128)} %pad.8.ids, s32[256,1]{1,0:T(8,128)} %copy.22.cluster, bf16[512,512]{1,0:T(8,128)(2,1)} %dst.1, bf16[512,512]{1,0:T(8,128)(2,1)} %src.3, ...), custom_call_target="tpu_custom_call" | custom-call | tf_op jit(solution)/shard_map/coarse/pallas_call | solution.py:156
  (12 shorter events, 0.3 us)
Async XLA Ops:
  0.0 28.4 %copy-start = (bf16[512,512]{1,0:T(8,128)(2,1)S(1)}, bf16[512,512]{1,0:T(8,128)(2,1)}, u32[]{:S(2)}) copy-start(bf16[512,512]{1,0:T(8,128)(2,1)} %param.22) | copy-start | bytes 1572868
  0.8 13.1 %copy-start.1 = (bf16[256,512]{1,0:T(8,128)(2,1)S(1)}, bf16[256,512]{1,0:T(8,128)(2,1)}, u32[]{:S(2)}) copy-start(bf16[256,512]{1,0:T(8,128)(2,1)} %features.1) | copy-start | bytes 786436
  2.0 13.4 %collective-permute-start = (bf16[272,512]{1,0:T(8,128)(2,1)S(1)}, bf16[272,512]{1,0:T(8,128)(2,1)S(1)}, u32[]{:S(2)}, u32[]{:S(2)}) collective-permute-start(bf16[272,512]{1,0:T(8,128)(2,1)S(1)} %maximum_maximum_fusion), channel_id=1, source_target_pairs={{0,496},{16,0},{32,16},{48,32},{64,48},{80,64},{96,80},{112,96},{1... | collective-permute-start | bytes 835592 | tf_op jit(solution)/shard_map/ppermute | solution.py:18
  10.1 12.5 %collective-permute-start.1 = (bf16[272,512]{1,0:T(8,128)(2,1)S(1)}, bf16[272,512]{1,0:T(8,128)(2,1)S(1)}, u32[]{:S(2)}, u32[]{:S(2)}) collective-permute-start(bf16[272,512]{1,0:T(8,128)(2,1)S(1)} %maximum_maximum_fusion), channel_id=1, source_target_pairs={{0,16},{16,32},{32,48},{48,64},{64,80},{80,96},{96,112},{112,128},... | collective-permute-start | bytes 835592 | tf_op jit(solution)/shard_map/ppermute | solution.py:18
  22.7 3.9 %copy-start.2 = (bf16[512,512]{1,0:T(8,128)(2,1)S(1)}, bf16[512,512]{1,0:T(8,128)(2,1)}, u32[]{:S(2)}) copy-start(bf16[512,512]{1,0:T(8,128)(2,1)} %src.2) | copy-start | bytes 1572868
  22.7 9.3 %collective-permute-start.3 = (bf16[384,512]{1,0:T(8,128)(2,1)S(1)}, bf16[384,512]{1,0:T(8,128)(2,1)S(1)}, u32[]{:S(2)}, u32[]{:S(2)}) collective-permute-start(bf16[384,512]{1,0:T(8,128)(2,1)S(1)} %pad_maximum_fusion.1), channel_id=1, source_target_pairs={{0,15},{1,0},{2,1},{3,2},{4,3},{5,4},{6,5},{7,6},{8,7},{9,8},{10,9... | collective-permute-start | bytes 1179656 | tf_op jit(solution)/shard_map/ppermute | solution.py:18
  24.6 8.6 %collective-permute-start.2 = (bf16[384,512]{1,0:T(8,128)(2,1)S(1)}, bf16[384,512]{1,0:T(8,128)(2,1)S(1)}, u32[]{:S(2)}, u32[]{:S(2)}) collective-permute-start(bf16[384,512]{1,0:T(8,128)(2,1)S(1)} %pad_maximum_fusion), channel_id=1, source_target_pairs={{0,1},{1,2},{2,3},{3,4},{4,5},{5,6},{6,7},{7,8},{8,9},{9,10},{10,1... | collective-permute-start | bytes 1179656 | tf_op jit(solution)/shard_map/ppermute | solution.py:18
  26.6 1.0 %copy-start.5 = (s32[6,256]{1,0:T(8,128)S(1)}, s32[6,256]{1,0:T(8,128)}, u32[]{:S(2)}) copy-start(s32[6,256]{1,0:T(8,128)} %param.18) | copy-start | bytes 18436
  27.8 0.7 slice-start
  32.0 1.2 %copy-start.3 = (bf16[384,512]{1,0:T(8,128)(2,1)}, bf16[384,512]{1,0:T(8,128)(2,1)S(1)}, u32[]{:S(2)}) copy-start(bf16[384,512]{1,0:T(8,128)(2,1)S(1)} %collective-permute-done.3.above) | copy-start | bytes 1179652
  33.2 0.7 copy-start.4
  63.9 8.6 %copy-start.6 = (s32[6,256]{1,0:T(8,128)S(1)}, s32[6,256]{1,0:T(8,128)}, u32[]{:S(2)}) copy-start(s32[6,256]{1,0:T(8,128)} %param.21) | copy-start | bytes 18436
  63.9 10.9 %collective-permute-start.4 = (bf16[16,512]{1,0:T(8,128)(2,1)S(1)}, bf16[16,512]{1,0:T(8,128)(2,1)S(1)}, u32[]{:S(2)}, u32[]{:S(2)}) collective-permute-start(bf16[16,512]{1,0:T(8,128)(2,1)S(1)} %multiply_convert_fusion), channel_id=1, source_target_pairs={{0,16},{16,32},{32,48},{48,64},{64,80},{80,96},{96,112},{112,128},... | collective-permute-start | bytes 49160 | tf_op jit(solution)/shard_map/ppermute | solution.py:18
  65.9 9.0 %collective-permute-start.5 = (bf16[16,512]{1,0:T(8,128)(2,1)S(1)}, bf16[16,512]{1,0:T(8,128)(2,1)S(1)}, u32[]{:S(2)}, u32[]{:S(2)}) collective-permute-start(bf16[16,512]{1,0:T(8,128)(2,1)S(1)} %multiply_convert_fusion), channel_id=1, source_target_pairs={{0,496},{16,0},{32,16},{48,32},{64,48},{80,64},{96,80},{112,96},{1... | collective-permute-start | bytes 49160 | tf_op jit(solution)/shard_map/ppermute | solution.py:18
  73.4 0.7 copy-start.7

commit v2 on v1

--- a/solution.py
+++ b/solution.py
@@ -8,6 +8,7 @@
 PATCH = 128
 POOL = 16
 META = 16
+GROUP = 2
 EPSILON = 1e-05
 F32 = jnp.float32
 BF16 = jnp.bfloat16
@@ -18,6 +19,10 @@
     return lax.ppermute(block, axis, [(i, (i + step) % count) for i in range(count)])
 
 
+def near(*arrays):
+    return [pltpu.with_memory_space_constraint(a, pltpu.VMEM) for a in arrays]
+
+
 def dot(left, right):
     return jnp.dot(left, right, preferred_element_type=F32)
 
@@ -25,6 +30,10 @@
 def one_hot(column, width, value):
     lanes = lax.broadcasted_iota(jnp.int32, (column.shape[0], width), 1)
     return jnp.where(column == lanes, F32(value), F32(0)).astype(BF16)
+
+
+def columns(index_rows):
+    return index_rows.astype(F32).T.astype(jnp.int32)
 
 
 def silu_of_half(half):
@@ -40,13 +49,33 @@
 
 def messages(ids, sources, target_half, edge, node, bias_half, gain):
     half_edge = edge * BF16(0.5)
+    rows = ids.shape[0]
     total = None
-    for e in range(6):
-        chosen = one_hot(ids[:, e : e + 1], sources.shape[0], 0.5)
-        hidden = silu_of_half(dot(chosen, sources) + target_half).astype(BF16)
-        signal = silu_of_half(dot(hidden, half_edge) + bias_half)
-        total = signal if total is None else total + signal
+    for e in range(0, 6, GROUP):
+        chosen = jnp.concatenate(
+            [one_hot(ids[:, k : k + 1], sources.shape[0], 0.5) for k in range(e, e + GROUP)], axis=0
+        )
+        picked = dot(chosen, sources)
+        hidden = jnp.concatenate(
+            [
+                silu_of_half(picked[k * rows : (k + 1) * rows] + target_half).astype(BF16)
+                for k in range(GROUP)
+            ],
+            axis=0,
+        )
+        signals = silu_of_half(dot(hidden, half_edge) + bias_half)
+        for k in range(GROUP):
+            signal = signals[k * rows : (k + 1) * rows]
+            total = signal if total is None else total + signal
     return gain * normalise(dot(total.astype(BF16), node))
+
+
+def listed_kernel(features, listing, out):
+    rows, width = features.shape
+    out[pl.ds(0, rows), :] = features[...]
+    lists = columns(jnp.broadcast_to(listing[...], (8, listing.shape[1])))[:, :1]
+    lists = jnp.broadcast_to(lists.astype(F32), (8, width))
+    out[pl.ds(rows, META), :] = jnp.concatenate([lists, jnp.zeros_like(lists)], axis=0).astype(BF16)
 
 
 def fine_kernel(
@@ -67,7 +96,7 @@
         for k, number in enumerate(numbers):
             place(number, projected[k * PATCH : (k + 1) * PATCH])
     update = messages(
-        ids[...], sources[...], target_half[...], edge[...], node[...], 0.5 * bias[1:2, :], gain[...]
+        columns(ids[...]), sources[...], target_half[...], edge[...], node[...], 0.5 * bias[1:2, :], gain[...]
     )
     fine_rows = (features[...].astype(F32) + update).astype(BF16)
     rows_out[...] = fine_rows
@@ -84,13 +113,14 @@
     clusters = pooled.shape[0]
     sources = dot(spread[...], src[...]).astype(BF16)
     target_half = 0.5 * (dot(pooled[...], dst[...]) + bias[0:1, :])
-    place = ids[...]
+    place = columns(ids[...])
     within = place & (clusters - 1)
     place = (within >> 4) * 48 + (place >> 8) * 16 + (within & 15)
     update = messages(
         place, sources, target_half, edge[...], node[...], 0.5 * bias[1:2, :], gain[...]
     ).astype(BF16)
-    lifted = dot(one_hot(cluster[...], clusters, 1.0), update)
+    owner = columns(jnp.broadcast_to(cluster[...], (8, cluster.shape[1])))[:, :1]
+    lifted = dot(one_hot(owner, clusters, 1.0), update)
     out[...] = (fine_rows[...].astype(F32) + lifted).astype(BF16)
 
 
@@ -117,8 +147,12 @@
     shares = lax.axis_size("gather")
     clusters = shares * rows // POOL
     share = clusters // shares
-    listing = jnp.broadcast_to(send_list.reshape(8, 1).astype(BF16), (8, width))
-    own = jnp.concatenate([features, listing, jnp.zeros((META - 8, width), BF16)], axis=0)
+    own = pl.pallas_call(
+        listed_kernel,
+        out_shape=pltpu.VMEM((rows + META, width), BF16),
+        compiler_params=pltpu.CompilerParams(vmem_limit_bytes=8 << 20),
+        name="listed",
+    )(features, send_list.reshape(1, 8))
     before = shifted(own, "section", 1)
     after = shifted(own, "section", -1)
 
@@ -127,8 +161,6 @@
 
     own_sources = dot(features, fine_src).astype(BF16)
     target_half = 0.5 * (dot(features, fine_dst) + fine_bias[0])
-    ids = jnp.pad(neighbours.T, ((0, 0), (0, 2)))
-    coarse_ids = jnp.pad(coarse_neighbours.T, ((0, 0), (0, 2)))
     to_next = jnp.concatenate([chosen(after, 2), chosen(own, 4), chosen(before, 7)], axis=0)
     to_last = jnp.concatenate([chosen(after, 0), chosen(own, 3), chosen(before, 5)], axis=0)
     below = shifted(to_next, "gather", 1)
@@ -138,15 +170,16 @@
     fine_rows, partial = pl.pallas_call(
         fine_kernel,
         out_shape=(
-            jax.ShapeDtypeStruct((rows, width), BF16),
-            jax.ShapeDtypeStruct((clusters, width), BF16),
+            pltpu.VMEM((rows, width), BF16),
+            pltpu.VMEM((clusters, width), BF16),
         ),
         scratch_shapes=[pltpu.VMEM((rows + 8 * PATCH, width), BF16)],
+        compiler_params=pltpu.CompilerParams(vmem_limit_bytes=24 << 20),
         name="fine",
-    )(
-        features, own_sources, target_half, beside, below, above, ids, cluster[None, :],
+    )(*near(
+        features, own_sources, target_half, beside, below, above, neighbours, cluster[None, :],
         fine_src, fine_edge, fine_node, fine_bias, fine_gain[None, :],
-    )
+    ))
 
     parts = lax.all_to_all(partial.reshape(shares, share, width), "gather", 0, 0, tiled=True)
     pooled = (jnp.sum(parts.astype(F32), axis=0) / POOL).astype(BF16)
@@ -157,11 +190,12 @@
         coarse_kernel,
         out_shape=jax.ShapeDtypeStruct((rows, width), BF16),
         scratch_shapes=[pltpu.VMEM((clusters, width), BF16)],
+        compiler_params=pltpu.CompilerParams(vmem_limit_bytes=24 << 20),
         name="coarse",
-    )(
-        spread, fine_rows, coarse_ids, cluster[:, None],
+    )(*near(
+        spread, fine_rows, coarse_neighbours, cluster[None, :],
         coarse_dst, coarse_src, coarse_edge, coarse_node, coarse_bias, coarse_gain[None, :],
-    )
+    ))
 
 
 def solution(mesh):

time: 100 us -> 93.2 us (0.932)
  Pallas kernels: 14.5 us -> 8.95 us
  starting transfers between devices: 22.5 us -> 26.1 us
  waiting for transfers between devices: 11.5 us -> 14.1 us
  other arithmetic: 2.87 us -> 0.32 us
  blocking collectives: 40.2 us -> 38.7 us
  matrix products: 2.09 us -> 0.6 us
  between operations: 1.44 us -> 0.25 us
    ppermute x6, starting transfers between devices: 22.5 us -> 26.1 us  [shifted(): lax.ppermute(block, axis, [(i, (i + step) % count) for i in range(count)])]
    pallas_call x1 -> x2, Pallas kernels: 7.73 us -> 4.49 us  [the longest x1 4.35 us: body(): pl.pallas_call(fine_kernel, out_shape=(pltpu.VMEM((rows, width), BF16), p...]
    ppermute x6, waiting for transfers between devices: 11.5 us -> 14.1 us  [shifted(): lax.ppermute(block, axis, [(i, (i + step) % count) for i in range(count)])]
    pallas_call x1, Pallas kernels: 6.8 us -> 4.46 us  [body(): pl.pallas_call(coarse_kernel, out_shape=jax.ShapeDtypeStruct((rows, width...]
    dot_general x2, matrix products: 2.09 us -> 0.6 us  [dot(): return jnp.dot(left, right, preferred_element_type=F32)]
    pad x2 -> x0, local copies, waits for them, and re-layouts: 1.32 us -> none  [the longest x1 0.66 us: body(): coarse_ids = jnp.pad(coarse_neighbours.T, ((0, 0), (0, 2)))]
    unnamed x18 -> x36, local copies, waits for them, and re-layouts: 1.72 us -> 3.02 us
    all_to_all x1, blocking collectives: 22.2 us -> 21 us  [body(): lax.all_to_all(partial.reshape(shares, share, width), 'gather', 0, 0, til...]
  transfers between devices with their start and end apart: 6 -> 6, of which waited for: 4 -> 5; matrix products, arithmetic and copies ran while one was open for 6% -> 1% of each run, Pallas kernels for 0% -> 0%
where the time goes in v2:
time: 93.2 us; the launch traced here: 92.8 us
  blocking collectives  38.7 us (42%)
  starting transfers between devices  26.1 us (28%)
  waiting for transfers between devices  14.1 us (15%)
  Pallas kernels  8.95 us (10%)
  local copies, waits for them, and re-layouts  3.69 us (4%)
    ppermute x6, starting transfers between devices, shifted(): lax.ppermute(block, axis, [(i, (i + step) % count) for i in range(count)])  26.1 us
    all_to_all x1, blocking collectives, body(): lax.all_to_all(partial.reshape(shares, share, width), 'gather', 0, 0, til...  21 us
    all_gather x1, blocking collectives, body(): lax.all_gather(jnp.concatenate(sides, axis=0), 'gather', axis=0, tiled=True)  17.7 us
    ppermute x6, waiting for transfers between devices, shifted(): lax.ppermute(block, axis, [(i, (i + step) % count) for i in range(count)])  14.1 us
    pallas_call x1, Pallas kernels, body(): pl.pallas_call(coarse_kernel, out_shape=jax.ShapeDtypeStruct((rows, width...  4.46 us
    pallas_call x1, Pallas kernels, body(): pl.pallas_call(fine_kernel, out_shape=(pltpu.VMEM((rows, width), BF16), p...  4.35 us
    unnamed x36, local copies, waits for them, and re-layouts  3.02 us
  transfers between devices with their start and end apart: 6, of which 5 were waited for; matrix products, arithmetic and copies ran while one was open for 1% of the time, Pallas kernels for 0%

profile of v2, /device:TPU:1, one launch (start us, length us, event | category | flops | bytes accessed | tf_op | source)
XLA Modules:
  0.0 92.8 jit_solution(8702366291172139152)
XLA Ops:
  0.0 0.0 copy-start
  0.0 0.7 copy-done.17
  0.7 0.0 copy-start.1
  0.7 0.9 %copy-done.1 = bf16[256,512]{1,0:T(8,128)(2,1)S(1)} copy-done((bf16[256,512]{1,0:T(8,128)(2,1)S(1)}, bf16[256,512]{1,0:T(8,128)(2,1)}, u32[]{:S(2)}) %copy-start.1) | copy-done | bytes 262168
  1.7 0.1 listed.1
  1.8 4.0 %collective-permute-start.1 = (bf16[272,512]{1,0:T(8,128)(2,1)S(1)}, bf16[272,512]{1,0:T(8,128)(2,1)S(1)}, u32[]{:S(2)}, u32[]{:S(2)}) collective-permute-start(bf16[272,512]{1,0:T(8,128)(2,1)S(1)} %listed.1), channel_id=1, source_target_pairs={{0,16},{16,32},{32,48},{48,64},{64,80},{80,96},{96,112},{112,128},... | collective-permute-start | bytes 835592 | tf_op jit(solution)/shard_map/ppermute | solution.py:19
  5.8 6.0 %collective-permute-start = (bf16[272,512]{1,0:T(8,128)(2,1)S(1)}, bf16[272,512]{1,0:T(8,128)(2,1)S(1)}, u32[]{:S(2)}, u32[]{:S(2)}) collective-permute-start(bf16[272,512]{1,0:T(8,128)(2,1)S(1)} %listed.1), channel_id=1, source_target_pairs={{0,496},{16,0},{32,16},{48,32},{64,48},{80,64},{96,80},{112,96},{1... | collective-permute-start | bytes 835592 | tf_op jit(solution)/shard_map/ppermute | solution.py:19
  11.9 1.9 %collective-permute-done.1 = bf16[272,512]{1,0:T(8,128)(2,1)S(1)} collective-permute-done((bf16[272,512]{1,0:T(8,128)(2,1)S(1)}, bf16[272,512]{1,0:T(8,128)(2,1)S(1)}, u32[]{:S(2)}, u32[]{:S(2)}) %collective-permute-start.1) | collective-permute-done | bytes 278560 | tf_op jit(solution)/shard_map/ppermute | solution.py:19
  13.9 1.4 %collective-permute-done = bf16[272,512]{1,0:T(8,128)(2,1)S(1)} collective-permute-done((bf16[272,512]{1,0:T(8,128)(2,1)S(1)}, bf16[272,512]{1,0:T(8,128)(2,1)S(1)}, u32[]{:S(2)}, u32[]{:S(2)}) %collective-permute-start) | collective-permute-done | bytes 278560 | tf_op jit(solution)/shard_map/ppermute | solution.py:19
  15.5 0.0 copy-start.3
  15.5 5.4 %collective-permute-start.2 = (bf16[384,512]{1,0:T(8,128)(2,1)S(1)}, bf16[384,512]{1,0:T(8,128)(2,1)S(1)}, u32[]{:S(2)}, u32[]{:S(2)}) collective-permute-start(bf16[384,512]{1,0:T(8,128)(2,1)S(1)} %pad_maximum_fusion), channel_id=1, source_target_pairs={{0,1},{1,2},{2,3},{3,4},{4,5},{5,6},{6,7},{7,8},{8,9},{9,10},{10,1... | collective-permute-start | bytes 1179656 | tf_op jit(solution)/shard_map/ppermute | solution.py:19
  20.8 0.0 copy-start.2
  20.9 1.2 %collective-permute-start.3 = (bf16[384,512]{1,0:T(8,128)(2,1)S(1)}, bf16[384,512]{1,0:T(8,128)(2,1)S(1)}, u32[]{:S(2)}, u32[]{:S(2)}) collective-permute-start(bf16[384,512]{1,0:T(8,128)(2,1)S(1)} %pad_maximum_fusion.1), channel_id=1, source_target_pairs={{0,15},{1,0},{2,1},{3,2},{4,3},{5,4},{6,5},{7,6},{8,7},{9,8},{10,9... | collective-permute-start | bytes 1179656 | tf_op jit(solution)/shard_map/ppermute | solution.py:19
  22.1 0.0 copy-done.3
  22.1 0.0 copy-done.2
  22.1 0.3 convolution_convert_fusion.own_sources
  22.4 0.0 slice-start
  22.4 0.0 copy-done
  22.4 0.7 slice-done
  23.1 0.3 fusion.target_half
  23.4 0.0 copy-start.4
  23.4 0.0 copy-start.10
  23.5 0.0 copy-start.15
  23.5 2.1 %collective-permute-done.2.below = bf16[384,512]{1,0:T(8,128)(2,1)S(1)} collective-permute-done((bf16[384,512]{1,0:T(8,128)(2,1)S(1)}, bf16[384,512]{1,0:T(8,128)(2,1)S(1)}, u32[]{:S(2)}, u32[]{:S(2)}) %collective-permute-start.2) | collective-permute-done | bytes 393248 | tf_op jit(solution)/shard_map/ppermute | solution.py:19
  25.6 2.8 %collective-permute-done.3.above = bf16[384,512]{1,0:T(8,128)(2,1)S(1)} collective-permute-done((bf16[384,512]{1,0:T(8,128)(2,1)S(1)}, bf16[384,512]{1,0:T(8,128)(2,1)S(1)}, u32[]{:S(2)}, u32[]{:S(2)}) %collective-permute-start.3) | collective-permute-done | bytes 393248 | tf_op jit(solution)/shard_map/ppermute | solution.py:19
  28.4 0.0 copy-done.5
  28.4 0.0 copy-done.11
  28.4 0.0 copy-done.4
  28.4 0.0 copy-done.10
  28.4 0.0 copy-done.15
  28.4 0.6 copy-done.14
  29.1 4.4 %fine.1 = (bf16[256,512]{1,0:T(8,128)(2,1)S(1)}, bf16[256,512]{1,0:T(8,128)(2,1)S(1)}) custom-call(bf16[256,512]{1,0:T(8,128)(2,1)S(1)} %copy-done.2, bf16[256,512]{1,0:T(8,128)(2,1)S(1)} %convolution_convert_fusion.own_sources, f32[256,512]{1,0:T(8,128)S(1)} %fusion.target_half, bf16[256,512]{1,0:T(8,128)(2,1)S(1)} %pad_maximum_fusion.2.beside, ...), custom_call_target="tpu_custom_call" | custom-call | tf_op jit(solution)/shard_map/fine/pallas_call | solution.py:170
  33.4 0.0 copy-start.8
  33.4 21.0 %all_to_all.5 = bf16[16,16,512]{2,1,0:T(8,128)(2,1)S(1)} all-to-all(bf16[16,16,512]{2,1,0:T(8,128)(2,1)S(1)} %bitcast.10), channel_id=1, replica_groups=mesh['section'=32,'gather'=16] {'gather'}, dimensions={0} | all-to-all | bytes 524288 | tf_op jit(solution)/shard_map/all_to_all | solution.py:184
  54.5 0.0 copy-start.6
  54.5 7.6 %collective-permute-start.5 = (bf16[16,512]{1,0:T(8,128)(2,1)S(1)}, bf16[16,512]{1,0:T(8,128)(2,1)S(1)}, u32[]{:S(2)}, u32[]{:S(2)}) collective-permute-start(bf16[16,512]{1,0:T(8,128)(2,1)S(1)} %multiply_convert_fusion), channel_id=1, source_target_pairs={{0,496},{16,0},{32,16},{48,32},{64,48},{80,64},{96,80},{112,96},{1... | collective-permute-start | bytes 49160 | tf_op jit(solution)/shard_map/ppermute | solution.py:19
  62.1 1.9 %collective-permute-start.4 = (bf16[16,512]{1,0:T(8,128)(2,1)S(1)}, bf16[16,512]{1,0:T(8,128)(2,1)S(1)}, u32[]{:S(2)}, u32[]{:S(2)}) collective-permute-start(bf16[16,512]{1,0:T(8,128)(2,1)S(1)} %multiply_convert_fusion), channel_id=1, source_target_pairs={{0,16},{16,32},{32,48},{48,64},{64,80},{80,96},{96,112},{112,128},... | collective-permute-start | bytes 49160 | tf_op jit(solution)/shard_map/ppermute | solution.py:19
  64.0 0.0 collective-permute-done.5
  64.1 5.9 %collective-permute-done.4 = bf16[16,512]{1,0:T(8,128)(2,1)S(1)} collective-permute-done((bf16[16,512]{1,0:T(8,128)(2,1)S(1)}, bf16[16,512]{1,0:T(8,128)(2,1)S(1)}, u32[]{:S(2)}, u32[]{:S(2)}) %collective-permute-start.4) | collective-permute-done | bytes 16416 | tf_op jit(solution)/shard_map/ppermute | solution.py:19
  69.9 17.7 %all_gather.3.spread = bf16[768,512]{1,0:T(8,128)(2,1)S(1)} all-gather(bf16[48,512]{1,0:T(8,128)(2,1)S(1)} %pad_maximum_fusion.3), channel_id=1, replica_groups=mesh['section'=32,'gather'=16] {'gather'}, dimensions={0}, use_global_device_ids=true | all-gather | bytes 835584 | tf_op jit(solution)/shard_map/all_gather | solution.py:187
  87.7 0.0 copy-done.9
  87.7 0.0 copy-done.8
  87.7 0.0 copy-done.7
  87.7 0.0 copy-done.6
  87.7 0.0 copy-done.12
  87.7 0.0 copy-done.13
  87.7 0.6 copy-done.16
  88.3 4.5 %coarse.1 = bf16[256,512]{1,0:T(8,128)(2,1)} custom-call(bf16[768,512]{1,0:T(8,128)(2,1)S(1)} %all_gather.3.spread, bf16[256,512]{1,0:T(8,128)(2,1)S(1)} %get-tuple-element.8.fine_rows, s32[6,256]{1,0:T(8,128)S(1)} %copy-done.12, s32[1,256]{1,0:T(1,128)S(1)} %bitcast.13, bf16[512,512]{1,0:T(8,128)(2,1)S(1)} %copy-done.6, bf16[512,512]{1,0:T(8,128)(2,1)S(1)} %copy-done.7, ...), custom_call_target="tpu_custom_call" | custom-call | tf_op jit(solution)/shard_map/coarse/pallas_call | solution.py:189
  (21 shorter events, 0.3 us)
Async XLA Ops:
  0.0 22.4 %copy-start = (bf16[512,512]{1,0:T(8,128)(2,1)S(1)}, bf16[512,512]{1,0:T(8,128)(2,1)}, u32[]{:S(2)}) copy-start(bf16[512,512]{1,0:T(8,128)(2,1)} %param.22) | copy-start | bytes 1572868
  0.0 0.7 copy-start.17
  0.7 0.9 %copy-start.1 = (bf16[256,512]{1,0:T(8,128)(2,1)S(1)}, bf16[256,512]{1,0:T(8,128)(2,1)}, u32[]{:S(2)}) copy-start(bf16[256,512]{1,0:T(8,128)(2,1)} %features.3) | copy-start | bytes 786436
  1.8 12.0 %collective-permute-start.1 = (bf16[272,512]{1,0:T(8,128)(2,1)S(1)}, bf16[272,512]{1,0:T(8,128)(2,1)S(1)}, u32[]{:S(2)}, u32[]{:S(2)}) collective-permute-start(bf16[272,512]{1,0:T(8,128)(2,1)S(1)} %listed.1), channel_id=1, source_target_pairs={{0,16},{16,32},{32,48},{48,64},{64,80},{80,96},{96,112},{112,128},... | collective-permute-start | bytes 835592 | tf_op jit(solution)/shard_map/ppermute | solution.py:19
  5.8 9.5 %collective-permute-start = (bf16[272,512]{1,0:T(8,128)(2,1)S(1)}, bf16[272,512]{1,0:T(8,128)(2,1)S(1)}, u32[]{:S(2)}, u32[]{:S(2)}) collective-permute-start(bf16[272,512]{1,0:T(8,128)(2,1)S(1)} %listed.1), channel_id=1, source_target_pairs={{0,496},{16,0},{32,16},{48,32},{64,48},{80,64},{96,80},{112,96},{1... | collective-permute-start | bytes 835592 | tf_op jit(solution)/shard_map/ppermute | solution.py:19
  15.5 6.6 %copy-start.3 = (bf16[512,512]{1,0:T(8,128)(2,1)S(1)}, bf16[512,512]{1,0:T(8,128)(2,1)}, u32[]{:S(2)}) copy-start(bf16[512,512]{1,0:T(8,128)(2,1)} %src.2) | copy-start | bytes 1572868
  15.5 10.1 %collective-permute-start.2 = (bf16[384,512]{1,0:T(8,128)(2,1)S(1)}, bf16[384,512]{1,0:T(8,128)(2,1)S(1)}, u32[]{:S(2)}, u32[]{:S(2)}) collective-permute-start(bf16[384,512]{1,0:T(8,128)(2,1)S(1)} %pad_maximum_fusion), channel_id=1, source_target_pairs={{0,1},{1,2},{2,3},{3,4},{4,5},{5,6},{6,7},{7,8},{8,9},{9,10},{10,1... | collective-permute-start | bytes 1179656 | tf_op jit(solution)/shard_map/ppermute | solution.py:19
  20.8 1.3 %copy-start.2 = (bf16[256,512]{1,0:T(8,128)(2,1)S(1)}, bf16[256,512]{1,0:T(8,128)(2,1)}, u32[]{:S(2)}) copy-start(bf16[256,512]{1,0:T(8,128)(2,1)} %features.3) | copy-start | bytes 786436
  20.9 7.5 %collective-permute-start.3 = (bf16[384,512]{1,0:T(8,128)(2,1)S(1)}, bf16[384,512]{1,0:T(8,128)(2,1)S(1)}, u32[]{:S(2)}, u32[]{:S(2)}) collective-permute-start(bf16[384,512]{1,0:T(8,128)(2,1)S(1)} %pad_maximum_fusion.1), channel_id=1, source_target_pairs={{0,15},{1,0},{2,1},{3,2},{4,3},{5,4},{6,5},{7,6},{8,7},{9,8},{10,9... | collective-permute-start | bytes 1179656 | tf_op jit(solution)/shard_map/ppermute | solution.py:19
  22.4 0.7 slice-start
  23.1 5.3 %copy-start.5 = (bf16[512,512]{1,0:T(8,128)(2,1)S(1)}, bf16[512,512]{1,0:T(8,128)(2,1)}, u32[]{:S(2)}) copy-start(bf16[512,512]{1,0:T(8,128)(2,1)} %node.2) | copy-start | bytes 1572868
  23.1 5.3 %copy-start.11 = (s32[6,256]{1,0:T(8,128)S(1)}, s32[6,256]{1,0:T(8,128)}, u32[]{:S(2)}) copy-start(s32[6,256]{1,0:T(8,128)} %ids.2) | copy-start | bytes 18436
  23.4 5.0 %copy-start.4 = (bf16[512,512]{1,0:T(8,128)(2,1)S(1)}, bf16[512,512]{1,0:T(8,128)(2,1)}, u32[]{:S(2)}) copy-start(bf16[512,512]{1,0:T(8,128)(2,1)} %edge.2) | copy-start | bytes 1572868
  23.4 5.0 %copy-start.10 = (f32[2,512]{1,0:T(2,128)S(1)}, f32[2,512]{1,0:T(2,128)}, u32[]{:S(2)}) copy-start(f32[2,512]{1,0:T(2,128)} %bias.2) | copy-start | bytes 12292
  23.5 4.9 %copy-start.15 = (f32[512]{0:T(512)S(1)}, f32[512]{0:T(512)}, u32[]{:S(2)}) copy-start(f32[512]{0:T(512)} %param.27) | copy-start | bytes 6148
  28.4 0.7 copy-start.14
  29.1 58.6 %copy-start.9 = (bf16[512,512]{1,0:T(8,128)(2,1)S(1)}, bf16[512,512]{1,0:T(8,128)(2,1)}, u32[]{:S(2)}) copy-start(bf16[512,512]{1,0:T(8,128)(2,1)} %node.3) | copy-start | bytes 1572868
  33.4 54.2 %copy-start.8 = (bf16[512,512]{1,0:T(8,128)(2,1)S(1)}, bf16[512,512]{1,0:T(8,128)(2,1)}, u32[]{:S(2)}) copy-start(bf16[512,512]{1,0:T(8,128)(2,1)} %edge.3) | copy-start | bytes 1572868
  54.5 33.2 %copy-start.7 = (bf16[512,512]{1,0:T(8,128)(2,1)S(1)}, bf16[512,512]{1,0:T(8,128)(2,1)}, u32[]{:S(2)}) copy-start(bf16[512,512]{1,0:T(8,128)(2,1)} %src.3) | copy-start | bytes 1572868
  54.5 33.1 %copy-start.6 = (bf16[512,512]{1,0:T(8,128)(2,1)S(1)}, bf16[512,512]{1,0:T(8,128)(2,1)}, u32[]{:S(2)}) copy-start(bf16[512,512]{1,0:T(8,128)(2,1)} %dst.1) | copy-start | bytes 1572868
  54.5 9.5 %collective-permute-start.5 = (bf16[16,512]{1,0:T(8,128)(2,1)S(1)}, bf16[16,512]{1,0:T(8,128)(2,1)S(1)}, u32[]{:S(2)}, u32[]{:S(2)}) collective-permute-start(bf16[16,512]{1,0:T(8,128)(2,1)S(1)} %multiply_convert_fusion), channel_id=1, source_target_pairs={{0,496},{16,0},{32,16},{48,32},{64,48},{80,64},{96,80},{112,96},{1... | collective-permute-start | bytes 49160 | tf_op jit(solution)/shard_map/ppermute | solution.py:19
  62.1 7.8 %collective-permute-start.4 = (bf16[16,512]{1,0:T(8,128)(2,1)S(1)}, bf16[16,512]{1,0:T(8,128)(2,1)S(1)}, u32[]{:S(2)}, u32[]{:S(2)}) collective-permute-start(bf16[16,512]{1,0:T(8,128)(2,1)S(1)} %multiply_convert_fusion), channel_id=1, source_target_pairs={{0,16},{16,32},{32,48},{48,64},{64,80},{80,96},{96,112},{112,128},... | collective-permute-start | bytes 49160 | tf_op jit(solution)/shard_map/ppermute | solution.py:19
  69.9 17.8 %copy-start.12 = (s32[6,256]{1,0:T(8,128)S(1)}, s32[6,256]{1,0:T(8,128)}, u32[]{:S(2)}) copy-start(s32[6,256]{1,0:T(8,128)} %ids.3) | copy-start | bytes 18436
  69.9 17.8 %copy-start.13 = (f32[2,512]{1,0:T(2,128)S(1)}, f32[2,512]{1,0:T(2,128)}, u32[]{:S(2)}) copy-start(f32[2,512]{1,0:T(2,128)} %bias.3) | copy-start | bytes 12292
  87.7 0.7 copy-start.16

commit v3 on v2

--- a/solution.py
+++ b/solution.py
@@ -17,6 +17,19 @@
 def shifted(block, axis, step):
     count = lax.axis_size(axis)
     return lax.ppermute(block, axis, [(i, (i + step) % count) for i in range(count)])
+
+
+def alternating(block):
+    sections, shares = lax.axis_size("section"), lax.axis_size("gather")
+    return lax.ppermute(
+        block,
+        ("section", "gather"),
+        [
+            (s * shares + g, (s + 1 - 2 * (g % 2)) % sections * shares + g)
+            for s in range(sections)
+            for g in range(shares)
+        ],
+    )
 
 
 def near(*arrays):
@@ -109,13 +122,16 @@
 def coarse_kernel(spread, fine_rows, ids, cluster, dst, src, edge, node, bias, gain, out, pooled):
     shares = spread.shape[0] // 48
     for k in range(shares):
-        pooled[pl.ds(16 * k, 16), :] = spread[pl.ds(48 * k + 16, 16), :]
+        pooled[pl.ds(16 * k, 16), :] = spread[pl.ds(48 * k, 16), :]
     clusters = pooled.shape[0]
     sources = dot(spread[...], src[...]).astype(BF16)
     target_half = 0.5 * (dot(pooled[...], dst[...]) + bias[0:1, :])
     place = columns(ids[...])
     within = place & (clusters - 1)
-    place = (within >> 4) * 48 + (place >> 8) * 16 + (within & 15)
+    section = place >> 8
+    own = (within >> 4) * 48 + (within & 15)
+    side = (within >> 5) * 96 + (within & 31) + 16
+    place = jnp.where(section == 1, own, side + (section >> 1) * 48)
     update = messages(
         place, sources, target_half, edge[...], node[...], 0.5 * bias[1:2, :], gain[...]
     ).astype(BF16)
@@ -152,7 +168,7 @@
         out_shape=pltpu.VMEM((rows + META, width), BF16),
         compiler_params=pltpu.CompilerParams(vmem_limit_bytes=8 << 20),
         name="listed",
-    )(features, send_list.reshape(1, 8))
+    )(*(pltpu.with_memory_space_constraint(a, pltpu.HBM) for a in (features, send_list.reshape(1, 8))))
     before = shifted(own, "section", 1)
     after = shifted(own, "section", -1)
 
@@ -183,8 +199,10 @@
 
     parts = lax.all_to_all(partial.reshape(shares, share, width), "gather", 0, 0, tiled=True)
     pooled = (jnp.sum(parts.astype(F32), axis=0) / POOL).astype(BF16)
-    sides = [shifted(pooled, "section", 1), pooled, shifted(pooled, "section", -1)]
-    spread = lax.all_gather(jnp.concatenate(sides, axis=0), "gather", axis=0, tiled=True)
+    pairs = [[2 * k, 2 * k + 1] for k in range(shares // 2)]
+    chip = lax.all_gather(pooled, "gather", axis=0, tiled=True, axis_index_groups=pairs)
+    side = alternating(chip)
+    spread = lax.all_gather(jnp.concatenate([pooled, side], axis=0), "gather", axis=0, tiled=True)
 
     return pl.pallas_call(
         coarse_kernel,

time: 93.2 us -> 87.7 us (0.941)
  waiting for transfers between devices: 14.1 us -> 9.28 us
  blocking collectives: 38.7 us -> 40.9 us
  starting transfers between devices: 26.1 us -> 24.1 us
  local copies, waits for them, and re-layouts: 3.69 us -> 2.02 us
  Pallas kernels: 8.95 us -> 9.96 us
    ppermute x6 -> x4, starting transfers between devices: 26.1 us -> 16.6 us  [shifted(): lax.ppermute(block, axis, [(i, (i + step) % count) for i in range(count)])]
    ppermute x0 -> x1, starting transfers between devices: none -> 7.42 us  [alternating(): lax.ppermute(block, ('section', 'gather'), [(s * shares + g, (s + 1 - 2 *...]
    ppermute x6 -> x4, waiting for transfers between devices: 14.1 us -> 8.27 us  [shifted(): lax.ppermute(block, axis, [(i, (i + step) % count) for i in range(count)])]
    all_gather x1 -> x2, blocking collectives: 17.7 us -> 19.9 us  [the longest x1 17.9 us: body(): lax.all_gather(jnp.concatenate([pooled, side], axis=0), 'gather', axis=0,...]
    unnamed x36 -> x32, local copies, waits for them, and re-layouts: 3.02 us -> 1.36 us
    pallas_call x1, Pallas kernels: 0.14 us -> 1.15 us  [body(): pl.pallas_call(listed_kernel, out_shape=pltpu.VMEM((rows + META, width),...]
    ppermute x0 -> x1, waiting for transfers between devices: none -> 1 us  [alternating(): lax.ppermute(block, ('section', 'gather'), [(s * shares + g, (s + 1 - 2 *...]
  transfers between devices with their start and end apart: 6 -> 5, of which waited for: 5 -> 5; matrix products, arithmetic and copies ran while one was open for 1% -> 1% of each run, Pallas kernels for 0% -> 0%
where the time goes in v3:
time: 87.7 us; the launch traced here: 87.4 us
  blocking collectives  40.9 us (47%)
  starting transfers between devices  24.1 us (27%)
  Pallas kernels  9.96 us (11%)
  waiting for transfers between devices  9.28 us (11%)
  local copies, waits for them, and re-layouts  2.02 us (2%)
    all_to_all x1, blocking collectives, body(): lax.all_to_all(partial.reshape(shares, share, width), 'gather', 0, 0, til...  21 us
    all_gather x1, blocking collectives, body(): lax.all_gather(jnp.concatenate([pooled, side], axis=0), 'gather', axis=0,...  17.9 us
    ppermute x4, starting transfers between devices, shifted(): lax.ppermute(block, axis, [(i, (i + step) % count) for i in range(count)])  16.6 us
    ppermute x4, waiting for transfers between devices, shifted(): lax.ppermute(block, axis, [(i, (i + step) % count) for i in range(count)])  8.27 us
    ppermute x1, starting transfers between devices, alternating(): lax.ppermute(block, ('section', 'gather'), [(s * shares + g, (s + 1 - 2 *...  7.42 us
    pallas_call x1, Pallas kernels, body(): pl.pallas_call(coarse_kernel, out_shape=jax.ShapeDtypeStruct((rows, width...  4.46 us
    pallas_call x1, Pallas kernels, body(): pl.pallas_call(fine_kernel, out_shape=(pltpu.VMEM((rows, width), BF16), p...  4.35 us
    all_gather x1, blocking collectives, body(): lax.all_gather(pooled, 'gather', axis=0, tiled=True, axis_index_groups=pa...  1.96 us
  transfers between devices with their start and end apart: 5, of which 5 were waited for; matrix products, arithmetic and copies ran while one was open for 1% of the time, Pallas kernels for 0%

profile of v3, /device:TPU:1, one launch (start us, length us, event | category | flops | bytes accessed | tf_op | source)
XLA Modules:
  0.0 87.4 jit_solution(11263640251440455745)
XLA Ops:
  0.0 0.0 copy-start
  0.0 1.1 %listed.1 = bf16[272,512]{1,0:T(8,128)(2,1)S(1)} custom-call(bf16[256,512]{1,0:T(8,128)(2,1)} %features.3, s32[1,8]{1,0:T(1,128)} %bitcast.16), custom_call_target="tpu_custom_call" | custom-call | tf_op jit(solution)/shard_map/listed/pallas_call | solution.py:166
  1.1 4.0 %collective-permute-start.1 = (bf16[272,512]{1,0:T(8,128)(2,1)S(1)}, bf16[272,512]{1,0:T(8,128)(2,1)S(1)}, u32[]{:S(2)}, u32[]{:S(2)}) collective-permute-start(bf16[272,512]{1,0:T(8,128)(2,1)S(1)} %listed.1), channel_id=1, source_target_pairs={{0,16},{16,32},{32,48},{48,64},{64,80},{80,96},{96,112},{112,128},... | collective-permute-start | bytes 835592 | tf_op jit(solution)/shard_map/ppermute | solution.py:19
  5.2 6.0 %collective-permute-start = (bf16[272,512]{1,0:T(8,128)(2,1)S(1)}, bf16[272,512]{1,0:T(8,128)(2,1)S(1)}, u32[]{:S(2)}, u32[]{:S(2)}) collective-permute-start(bf16[272,512]{1,0:T(8,128)(2,1)S(1)} %listed.1), channel_id=1, source_target_pairs={{0,496},{16,0},{32,16},{48,32},{64,48},{80,64},{96,80},{112,96},{1... | collective-permute-start | bytes 835592 | tf_op jit(solution)/shard_map/ppermute | solution.py:19
  11.3 1.9 %collective-permute-done.1 = bf16[272,512]{1,0:T(8,128)(2,1)S(1)} collective-permute-done((bf16[272,512]{1,0:T(8,128)(2,1)S(1)}, bf16[272,512]{1,0:T(8,128)(2,1)S(1)}, u32[]{:S(2)}, u32[]{:S(2)}) %collective-permute-start.1) | collective-permute-done | bytes 278560 | tf_op jit(solution)/shard_map/ppermute | solution.py:19
  13.2 1.4 %collective-permute-done = bf16[272,512]{1,0:T(8,128)(2,1)S(1)} collective-permute-done((bf16[272,512]{1,0:T(8,128)(2,1)S(1)}, bf16[272,512]{1,0:T(8,128)(2,1)S(1)}, u32[]{:S(2)}, u32[]{:S(2)}) %collective-permute-start) | collective-permute-done | bytes 278560 | tf_op jit(solution)/shard_map/ppermute | solution.py:19
  14.8 0.0 copy-start.2
  14.8 5.4 %collective-permute-start.2 = (bf16[384,512]{1,0:T(8,128)(2,1)S(1)}, bf16[384,512]{1,0:T(8,128)(2,1)S(1)}, u32[]{:S(2)}, u32[]{:S(2)}) collective-permute-start(bf16[384,512]{1,0:T(8,128)(2,1)S(1)} %pad_maximum_fusion), channel_id=1, source_target_pairs={{0,1},{1,2},{2,3},{3,4},{4,5},{5,6},{6,7},{7,8},{8,9},{9,10},{10,1... | collective-permute-start | bytes 1179656 | tf_op jit(solution)/shard_map/ppermute | solution.py:19
  20.2 0.0 copy-start.1
  20.2 1.2 %collective-permute-start.3 = (bf16[384,512]{1,0:T(8,128)(2,1)S(1)}, bf16[384,512]{1,0:T(8,128)(2,1)S(1)}, u32[]{:S(2)}, u32[]{:S(2)}) collective-permute-start(bf16[384,512]{1,0:T(8,128)(2,1)S(1)} %pad_maximum_fusion.1), channel_id=1, source_target_pairs={{0,15},{1,0},{2,1},{3,2},{4,3},{5,4},{6,5},{7,6},{8,7},{9,8},{10,9... | collective-permute-start | bytes 1179656 | tf_op jit(solution)/shard_map/ppermute | solution.py:19
  21.5 0.0 copy-done.2
  21.5 0.0 copy-done.1
  21.5 0.3 convolution_convert_fusion.own_sources
  21.8 0.0 slice-start
  21.8 0.0 copy-done
  21.8 0.7 slice-done
  22.5 0.0 copy-start.4
  22.5 0.0 copy-start.10
  22.5 0.3 fusion.target_half
  22.8 0.0 copy-start.3
  22.8 0.0 copy-start.9
  22.8 0.0 copy-start.14
  22.8 2.1 %collective-permute-done.2.below = bf16[384,512]{1,0:T(8,128)(2,1)S(1)} collective-permute-done((bf16[384,512]{1,0:T(8,128)(2,1)S(1)}, bf16[384,512]{1,0:T(8,128)(2,1)S(1)}, u32[]{:S(2)}, u32[]{:S(2)}) %collective-permute-start.2) | collective-permute-done | bytes 393248 | tf_op jit(solution)/shard_map/ppermute | solution.py:19
  24.9 2.8 %collective-permute-done.3.above = bf16[384,512]{1,0:T(8,128)(2,1)S(1)} collective-permute-done((bf16[384,512]{1,0:T(8,128)(2,1)S(1)}, bf16[384,512]{1,0:T(8,128)(2,1)S(1)}, u32[]{:S(2)}, u32[]{:S(2)}) %collective-permute-start.3) | collective-permute-done | bytes 393248 | tf_op jit(solution)/shard_map/ppermute | solution.py:19
  27.8 0.0 copy-start.13
  27.8 0.0 copy-done.4
  27.8 0.0 copy-done.10
  27.8 0.0 copy-done.3
  27.8 0.0 copy-done.9
  27.8 0.0 copy-done.14
  27.8 0.6 copy-done.13
  28.4 0.0 copy-start.8
  28.4 4.4 %fine.1 = (bf16[256,512]{1,0:T(8,128)(2,1)S(1)}, bf16[256,512]{1,0:T(8,128)(2,1)S(1)}) custom-call(bf16[256,512]{1,0:T(8,128)(2,1)S(1)} %copy-done.1, bf16[256,512]{1,0:T(8,128)(2,1)S(1)} %convolution_convert_fusion.own_sources, f32[256,512]{1,0:T(8,128)S(1)} %fusion.target_half, bf16[256,512]{1,0:T(8,128)(2,1)S(1)} %pad_maximum_fusion.2.beside, ...), custom_call_target="tpu_custom_call" | custom-call | tf_op jit(solution)/shard_map/fine/pallas_call | solution.py:186
  32.8 0.0 copy-start.7
  32.8 21.0 %all_to_all.5 = bf16[16,16,512]{2,1,0:T(8,128)(2,1)S(1)} all-to-all(bf16[16,16,512]{2,1,0:T(8,128)(2,1)S(1)} %bitcast.10), channel_id=1, replica_groups=mesh['section'=32,'gather'=16] {'gather'}, dimensions={0} | all-to-all | bytes 524288 | tf_op jit(solution)/shard_map/all_to_all | solution.py:200
  53.9 0.0 copy-start.5
  53.9 2.0 %all_gather.6 = bf16[32,512]{1,0:T(8,128)(2,1)S(1)} all-gather(bf16[16,512]{1,0:T(8,128)(2,1)S(1)} %multiply_convert_fusion), channel_id=1, replica_groups={{0,1},{2,3},{4,5},{6,7},{8,9},{10,11},{12,13},{14,15},{16,17},{18,19},{..., dimensions={0}, use_global_device_ids=true | all-gather | bytes 49152 | tf_op jit(solution)/shard_map/all_gather | solution.py:203
  55.9 7.4 %collective-permute-start.4 = (bf16[32,512]{1,0:T(8,128)(2,1)S(1)}, bf16[32,512]{1,0:T(8,128)(2,1)S(1)}, u32[]{:S(2)}, u32[]{:S(2)}) collective-permute-start(bf16[32,512]{1,0:T(8,128)(2,1)S(1)} %all_gather.6), channel_id=1, source_target_pairs={{0,16},{1,497},{2,18},{3,499},{4,20},{5,501},{6,22},{7,503},{8,24}... | collective-permute-start | bytes 98312 | tf_op jit(solution)/shard_map/ppermute | solution.py:24
  63.3 1.0 %collective-permute-done.4 = bf16[32,512]{1,0:T(8,128)(2,1)S(1)} collective-permute-done((bf16[32,512]{1,0:T(8,128)(2,1)S(1)}, bf16[32,512]{1,0:T(8,128)(2,1)S(1)}, u32[]{:S(2)}, u32[]{:S(2)}) %collective-permute-start.4) | collective-permute-done | bytes 32800 | tf_op jit(solution)/shard_map/ppermute | solution.py:24
  64.3 17.9 %all_gather.7.spread = bf16[768,512]{1,0:T(8,128)(2,1)S(1)} all-gather(bf16[48,512]{1,0:T(8,128)(2,1)S(1)} %pad_maximum_fusion.3), channel_id=1, replica_groups=mesh['section'=32,'gather'=16] {'gather'}, dimensions={0}, use_global_device_ids=true | all-gather | bytes 835584 | tf_op jit(solution)/shard_map/all_gather | solution.py:205
  82.2 0.0 copy-done.8
  82.2 0.0 copy-done.7
  82.2 0.0 copy-done.6
  82.2 0.0 copy-done.5
  82.3 0.0 copy-done.11
  82.3 0.0 copy-done.12
  82.3 0.6 copy-done.15
  82.9 4.5 %coarse.1 = bf16[256,512]{1,0:T(8,128)(2,1)} custom-call(bf16[768,512]{1,0:T(8,128)(2,1)S(1)} %all_gather.7.spread, bf16[256,512]{1,0:T(8,128)(2,1)S(1)} %get-tuple-element.8.fine_rows, s32[6,256]{1,0:T(8,128)S(1)} %copy-done.11, s32[1,256]{1,0:T(1,128)S(1)} %bitcast.13, bf16[512,512]{1,0:T(8,128)(2,1)S(1)} %copy-done.5, bf16[512,512]{1,0:T(8,128)(2,1)S(1)} %copy-done.6, ...), custom_call_target="tpu_custom_call" | custom-call | tf_op jit(solution)/shard_map/coarse/pallas_call | solution.py:207
  (16 shorter events, 0.3 us)
Async XLA Ops:
  0.0 21.8 %copy-start = (bf16[512,512]{1,0:T(8,128)(2,1)S(1)}, bf16[512,512]{1,0:T(8,128)(2,1)}, u32[]{:S(2)}) copy-start(bf16[512,512]{1,0:T(8,128)(2,1)} %param.22) | copy-start | bytes 1572868
  1.1 12.0 %collective-permute-start.1 = (bf16[272,512]{1,0:T(8,128)(2,1)S(1)}, bf16[272,512]{1,0:T(8,128)(2,1)S(1)}, u32[]{:S(2)}, u32[]{:S(2)}) collective-permute-start(bf16[272,512]{1,0:T(8,128)(2,1)S(1)} %listed.1), channel_id=1, source_target_pairs={{0,16},{16,32},{32,48},{48,64},{64,80},{80,96},{96,112},{112,128},... | collective-permute-start | bytes 835592 | tf_op jit(solution)/shard_map/ppermute | solution.py:19
  5.2 9.5 %collective-permute-start = (bf16[272,512]{1,0:T(8,128)(2,1)S(1)}, bf16[272,512]{1,0:T(8,128)(2,1)S(1)}, u32[]{:S(2)}, u32[]{:S(2)}) collective-permute-start(bf16[272,512]{1,0:T(8,128)(2,1)S(1)} %listed.1), channel_id=1, source_target_pairs={{0,496},{16,0},{32,16},{48,32},{64,48},{80,64},{96,80},{112,96},{1... | collective-permute-start | bytes 835592 | tf_op jit(solution)/shard_map/ppermute | solution.py:19
  14.8 6.6 %copy-start.2 = (bf16[512,512]{1,0:T(8,128)(2,1)S(1)}, bf16[512,512]{1,0:T(8,128)(2,1)}, u32[]{:S(2)}) copy-start(bf16[512,512]{1,0:T(8,128)(2,1)} %src.2) | copy-start | bytes 1572868
  14.8 10.1 %collective-permute-start.2 = (bf16[384,512]{1,0:T(8,128)(2,1)S(1)}, bf16[384,512]{1,0:T(8,128)(2,1)S(1)}, u32[]{:S(2)}, u32[]{:S(2)}) collective-permute-start(bf16[384,512]{1,0:T(8,128)(2,1)S(1)} %pad_maximum_fusion), channel_id=1, source_target_pairs={{0,1},{1,2},{2,3},{3,4},{4,5},{5,6},{6,7},{7,8},{8,9},{9,10},{10,1... | collective-permute-start | bytes 1179656 | tf_op jit(solution)/shard_map/ppermute | solution.py:19
  20.2 1.3 %copy-start.1 = (bf16[256,512]{1,0:T(8,128)(2,1)S(1)}, bf16[256,512]{1,0:T(8,128)(2,1)}, u32[]{:S(2)}) copy-start(bf16[256,512]{1,0:T(8,128)(2,1)} %features.3) | copy-start | bytes 786436
  20.2 7.5 %collective-permute-start.3 = (bf16[384,512]{1,0:T(8,128)(2,1)S(1)}, bf16[384,512]{1,0:T(8,128)(2,1)S(1)}, u32[]{:S(2)}, u32[]{:S(2)}) collective-permute-start(bf16[384,512]{1,0:T(8,128)(2,1)S(1)} %pad_maximum_fusion.1), channel_id=1, source_target_pairs={{0,15},{1,0},{2,1},{3,2},{4,3},{5,4},{6,5},{7,6},{8,7},{9,8},{10,9... | collective-permute-start | bytes 1179656 | tf_op jit(solution)/shard_map/ppermute | solution.py:19
  21.8 0.7 slice-start
  22.5 5.3 %copy-start.4 = (bf16[512,512]{1,0:T(8,128)(2,1)S(1)}, bf16[512,512]{1,0:T(8,128)(2,1)}, u32[]{:S(2)}) copy-start(bf16[512,512]{1,0:T(8,128)(2,1)} %node.2) | copy-start | bytes 1572868
  22.5 5.3 %copy-start.10 = (s32[6,256]{1,0:T(8,128)S(1)}, s32[6,256]{1,0:T(8,128)}, u32[]{:S(2)}) copy-start(s32[6,256]{1,0:T(8,128)} %ids.2) | copy-start | bytes 18436
  22.8 5.0 %copy-start.3 = (bf16[512,512]{1,0:T(8,128)(2,1)S(1)}, bf16[512,512]{1,0:T(8,128)(2,1)}, u32[]{:S(2)}) copy-start(bf16[512,512]{1,0:T(8,128)(2,1)} %edge.2) | copy-start | bytes 1572868
  22.8 5.0 %copy-start.9 = (f32[2,512]{1,0:T(2,128)S(1)}, f32[2,512]{1,0:T(2,128)}, u32[]{:S(2)}) copy-start(f32[2,512]{1,0:T(2,128)} %bias.2) | copy-start | bytes 12292
  22.8 4.9 %copy-start.14 = (f32[512]{0:T(512)S(1)}, f32[512]{0:T(512)}, u32[]{:S(2)}) copy-start(f32[512]{0:T(512)} %param.27) | copy-start | bytes 6148
  27.8 0.7 copy-start.13
  28.4 53.8 %copy-start.8 = (bf16[512,512]{1,0:T(8,128)(2,1)S(1)}, bf16[512,512]{1,0:T(8,128)(2,1)}, u32[]{:S(2)}) copy-start(bf16[512,512]{1,0:T(8,128)(2,1)} %node.3) | copy-start | bytes 1572868
  32.8 49.4 %copy-start.7 = (bf16[512,512]{1,0:T(8,128)(2,1)S(1)}, bf16[512,512]{1,0:T(8,128)(2,1)}, u32[]{:S(2)}) copy-start(bf16[512,512]{1,0:T(8,128)(2,1)} %edge.3) | copy-start | bytes 1572868
  53.8 28.4 %copy-start.6 = (bf16[512,512]{1,0:T(8,128)(2,1)S(1)}, bf16[512,512]{1,0:T(8,128)(2,1)}, u32[]{:S(2)}) copy-start(bf16[512,512]{1,0:T(8,128)(2,1)} %src.3) | copy-start | bytes 1572868
  53.9 28.4 %copy-start.5 = (bf16[512,512]{1,0:T(8,128)(2,1)S(1)}, bf16[512,512]{1,0:T(8,128)(2,1)}, u32[]{:S(2)}) copy-start(bf16[512,512]{1,0:T(8,128)(2,1)} %dst.1) | copy-start | bytes 1572868
  55.9 8.4 %collective-permute-start.4 = (bf16[32,512]{1,0:T(8,128)(2,1)S(1)}, bf16[32,512]{1,0:T(8,128)(2,1)S(1)}, u32[]{:S(2)}, u32[]{:S(2)}) collective-permute-start(bf16[32,512]{1,0:T(8,128)(2,1)S(1)} %all_gather.6), channel_id=1, source_target_pairs={{0,16},{1,497},{2,18},{3,499},{4,20},{5,501},{6,22},{7,503},{8,24}... | collective-permute-start | bytes 98312 | tf_op jit(solution)/shard_map/ppermute | solution.py:24
  64.3 18.0 %copy-start.11 = (s32[6,256]{1,0:T(8,128)S(1)}, s32[6,256]{1,0:T(8,128)}, u32[]{:S(2)}) copy-start(s32[6,256]{1,0:T(8,128)} %ids.3) | copy-start | bytes 18436
  64.3 18.0 %copy-start.12 = (f32[2,512]{1,0:T(2,128)S(1)}, f32[2,512]{1,0:T(2,128)}, u32[]{:S(2)}) copy-start(f32[2,512]{1,0:T(2,128)} %bias.3) | copy-start | bytes 12292
  82.2 0.7 copy-start.15

commit v4 on v3

--- a/solution.py
+++ b/solution.py
@@ -4,6 +4,7 @@
 from jax.experimental import pallas as pl
 from jax.experimental.pallas import tpu as pltpu
 from jax.sharding import PartitionSpec as P
+
 
 PATCH = 128
 POOL = 16
@@ -32,8 +33,17 @@
     )
 
 
+def across_chip(block):
+    pairs = [[g, g + 1] for g in range(0, lax.axis_size("gather"), 2)]
+    return lax.all_gather(block, "gather", axis=0, tiled=True, axis_index_groups=pairs)
+
+
 def near(*arrays):
     return [pltpu.with_memory_space_constraint(a, pltpu.VMEM) for a in arrays]
+
+
+def far(*arrays):
+    return [pltpu.with_memory_space_constraint(a, pltpu.HBM) for a in arrays]
 
 
 def dot(left, right):
@@ -60,18 +70,30 @@
     return centred * lax.rsqrt(spread + EPSILON)
 
 
-def messages(ids, sources, target_half, edge, node, bias_half, gain):
-    half_edge = edge * BF16(0.5)
-    rows = ids.shape[0]
-    total = None
+def placed_rows(ids, numbers):
+    block = ids >> 7
+    place = jnp.full_like(ids, -1)
+    for k, number in enumerate(numbers):
+        place = jnp.where(block == number, ids - 128 * (number - k), place)
+    return place
+
+
+def edges_of(ids, sources):
     for e in range(0, 6, GROUP):
         chosen = jnp.concatenate(
             [one_hot(ids[:, k : k + 1], sources.shape[0], 0.5) for k in range(e, e + GROUP)], axis=0
         )
-        picked = dot(chosen, sources)
+        yield dot(chosen, sources)
+
+
+def messages(picked_halves, base_of, edge, node, bias_half, gain):
+    half_edge = edge * BF16(0.5)
+    total = None
+    for group, picked in enumerate(picked_halves):
+        rows = picked.shape[0] // GROUP
         hidden = jnp.concatenate(
             [
-                silu_of_half(picked[k * rows : (k + 1) * rows] + target_half).astype(BF16)
+                silu_of_half(picked[k * rows : (k + 1) * rows] + base_of(group * GROUP + k)).astype(BF16)
                 for k in range(GROUP)
             ],
             axis=0,
@@ -91,27 +113,56 @@
     out[pl.ds(rows, META), :] = jnp.concatenate([lists, jnp.zeros_like(lists)], axis=0).astype(BF16)
 
 
+def pick(block, number):
+    rows = block.shape[0] - META
+    listed = block[pl.ds(rows, META), :][number : number + 1, :]
+    later = jnp.broadcast_to(listed, (PATCH, block.shape[1])) > BF16(0.5)
+    return jnp.where(later, block[pl.ds(PATCH, PATCH), :], block[pl.ds(0, PATCH), :])
+
+
+def pick_kernel(own, to_next, to_last):
+    to_next[...] = pick(own, 4)
+    to_last[...] = pick(own, 3)
+
+
+def bundle_kernel(before, after, to_next, to_last, beside):
+    for out, of_after, of_before in ((to_next, 2, 7), (to_last, 0, 5), (beside, 1, 6)):
+        out[pl.ds(0, PATCH), :] = pick(after, of_after)
+        out[pl.ds(PATCH, PATCH), :] = pick(before, of_before)
+
+
+def mine_kernel(own, ids, dst, src, bias, own_sources, target_half, src_out, early_place, late_place):
+    rows = own_sources.shape[0]
+    features = own[pl.ds(0, rows), :]
+    own_sources[...] = dot(features, src[...]).astype(BF16)
+    target_half[...] = 0.5 * (dot(features, dst[...]) + bias[0:1, :])
+    src_out[...] = src[...]
+    early_place[...] = columns(placed_rows(ids[...], (0, 1, 3, 8)))
+    late_place[...] = columns(placed_rows(ids[...], (5, 6, 2, 7, 4, 9)))
+
+
+def early_kernel(own_sources, target_half, beside, place, src, base):
+    rows = own_sources.shape[0]
+    near_sources = dot(beside[...], src[...]).astype(BF16)
+    sources = jnp.concatenate([own_sources[...], near_sources], axis=0)
+    half = target_half[...]
+    for group, picked in enumerate(edges_of(place[...], sources)):
+        for k in range(GROUP):
+            base[pl.ds((group * GROUP + k) * rows, rows), :] = picked[k * rows : (k + 1) * rows] + half
+
+
 def fine_kernel(
-    features, own_sources, target_half, beside, below, above, ids, cluster, src, edge, node, bias, gain,
-    rows_out, partial_out, sources,
+    own, base, below_own, above_own, below, above, place, cluster, src, edge, node, bias, gain, rows_out, partial_out
 ):
-    rows = features.shape[0]
-
-    def place(number, value):
-        sources[pl.ds(rows + PATCH * number, PATCH), :] = value
-
-    sources[pl.ds(0, rows), :] = own_sources[...]
-    near = dot(beside[...], src[...]).astype(BF16)
-    place(1, near[:PATCH])
-    place(6, near[PATCH:])
-    for piece, numbers in ((above, (0, 3, 5)), (below, (2, 4, 7))):
-        projected = dot(piece[...], src[...]).astype(BF16)
-        for k, number in enumerate(numbers):
-            place(number, projected[k * PATCH : (k + 1) * PATCH])
+    rows = rows_out.shape[0]
+    pieces = (above_own, below_own, above, below)
+    sources = jnp.concatenate([dot(piece[...], src[...]).astype(BF16) for piece in pieces], axis=0)
     update = messages(
-        columns(ids[...]), sources[...], target_half[...], edge[...], node[...], 0.5 * bias[1:2, :], gain[...]
+        edges_of(place[...], sources),
+        lambda e: base[pl.ds(e * rows, rows), :],
+        edge[...], node[...], 0.5 * bias[1:2, :], gain[...],
     )
-    fine_rows = (features[...].astype(F32) + update).astype(BF16)
+    fine_rows = (own[pl.ds(0, rows), :].astype(F32) + update).astype(BF16)
     rows_out[...] = fine_rows
     clusters = partial_out.shape[0]
     member = lax.broadcasted_iota(jnp.int32, (clusters, rows), 0) == cluster[...]
@@ -133,7 +184,7 @@
     side = (within >> 5) * 96 + (within & 31) + 16
     place = jnp.where(section == 1, own, side + (section >> 1) * 48)
     update = messages(
-        place, sources, target_half, edge[...], node[...], 0.5 * bias[1:2, :], gain[...]
+        edges_of(place, sources), lambda e: target_half, edge[...], node[...], 0.5 * bias[1:2, :], gain[...]
     ).astype(BF16)
     owner = columns(jnp.broadcast_to(cluster[...], (8, cluster.shape[1])))[:, :1]
     lifted = dot(one_hot(owner, clusters, 1.0), update)
@@ -168,20 +219,43 @@
         out_shape=pltpu.VMEM((rows + META, width), BF16),
         compiler_params=pltpu.CompilerParams(vmem_limit_bytes=8 << 20),
         name="listed",
-    )(*(pltpu.with_memory_space_constraint(a, pltpu.HBM) for a in (features, send_list.reshape(1, 8))))
+    )(*far(features, send_list.reshape(1, 8)))
     before = shifted(own, "section", 1)
     after = shifted(own, "section", -1)
 
-    def chosen(block, number):
-        return jnp.where(block[rows + number][None, :] > 0.5, block[PATCH:rows], block[:PATCH])
-
-    own_sources = dot(features, fine_src).astype(BF16)
-    target_half = 0.5 * (dot(features, fine_dst) + fine_bias[0])
-    to_next = jnp.concatenate([chosen(after, 2), chosen(own, 4), chosen(before, 7)], axis=0)
-    to_last = jnp.concatenate([chosen(after, 0), chosen(own, 3), chosen(before, 5)], axis=0)
+    small = pltpu.CompilerParams(vmem_limit_bytes=8 << 20)
+    up, down = pl.pallas_call(
+        pick_kernel, out_shape=(pltpu.VMEM((PATCH, width), BF16),) * 2, compiler_params=small, name="pick"
+    )(*near(own))
+    below_own = shifted(up, "gather", 1)
+    above_own = shifted(down, "gather", -1)
+    to_next, to_last, beside = pl.pallas_call(
+        bundle_kernel,
+        out_shape=(pltpu.VMEM((2 * PATCH, width), BF16),) * 3,
+        compiler_params=small,
+        name="bundle",
+    )(*near(before, after))
     below = shifted(to_next, "gather", 1)
     above = shifted(to_last, "gather", -1)
-    beside = jnp.concatenate([chosen(after, 1), chosen(before, 6)], axis=0)
+
+    own_sources, target_half, fine_src, early_place, late_place = pl.pallas_call(
+        mine_kernel,
+        out_shape=(
+            pltpu.VMEM((rows, width), BF16),
+            pltpu.VMEM((rows, width), F32),
+            pltpu.VMEM((width, width), BF16),
+            pltpu.VMEM((rows, 6), jnp.int32),
+            pltpu.VMEM((rows, 6), jnp.int32),
+        ),
+        compiler_params=small,
+        name="mine",
+    )(*near(own), *far(neighbours, fine_dst, fine_src, fine_bias))
+    base = pl.pallas_call(
+        early_kernel,
+        out_shape=pltpu.VMEM((6 * rows, width), F32),
+        compiler_params=pltpu.CompilerParams(vmem_limit_bytes=24 << 20),
+        name="early",
+    )(*near(own_sources, target_half, beside, early_place, fine_src))
 
     fine_rows, partial = pl.pallas_call(
         fine_kernel,
@@ -189,19 +263,16 @@
             pltpu.VMEM((rows, width), BF16),
             pltpu.VMEM((clusters, width), BF16),
         ),
-        scratch_shapes=[pltpu.VMEM((rows + 8 * PATCH, width), BF16)],
         compiler_params=pltpu.CompilerParams(vmem_limit_bytes=24 << 20),
         name="fine",
     )(*near(
-        features, own_sources, target_half, beside, below, above, neighbours, cluster[None, :],
+        own, base, below_own, above_own, below, above, late_place, cluster[None, :],
         fine_src, fine_edge, fine_node, fine_bias, fine_gain[None, :],
     ))
 
     parts = lax.all_to_all(partial.reshape(shares, share, width), "gather", 0, 0, tiled=True)
     pooled = (jnp.sum(parts.astype(F32), axis=0) / POOL).astype(BF16)
-    pairs = [[2 * k, 2 * k + 1] for k in range(shares // 2)]
-    chip = lax.all_gather(pooled, "gather", axis=0, tiled=True, axis_index_groups=pairs)
-    side = alternating(chip)
+    side = alternating(across_chip(pooled))
     spread = lax.all_gather(jnp.concatenate([pooled, side], axis=0), "gather", axis=0, tiled=True)
 
     return pl.pallas_call(
@@ -224,6 +295,5 @@
         P(("section", "gather")),
         P(None, "section"),
     ) + (P(),) * 12
-    return jax.shard_map(
-        body, mesh=mesh, in_specs=placed, out_specs=P(("section", "gather"), None), check_vma=False
-    )
+
+    return jax.shard_map(body, mesh=mesh, in_specs=placed, out_specs=P(("section", "gather"), None), check_vma=False)

time: 87.7 us -> 85.2 us (0.971)
  waiting for transfers between devices: 9.28 us -> 4.48 us
  starting transfers between devices: 24.1 us -> 28.5 us
  local copies, waits for them, and re-layouts: 2.02 us -> 0.08 us
  Pallas kernels: 9.96 us -> 11.9 us
  blocking collectives: 40.9 us -> 39.6 us
    ppermute x4 -> x6, waiting for transfers between devices: 8.27 us -> 3.48 us  [shifted(): lax.ppermute(block, axis, [(i, (i + step) % count) for i in range(count)])]
    ppermute x4 -> x6, starting transfers between devices: 16.6 us -> 21.1 us  [shifted(): lax.ppermute(block, axis, [(i, (i + step) % count) for i in range(count)])]
    pallas_call x0 -> x4, Pallas kernels: none -> 2.9 us  [the longest x1 1.67 us: body(): pl.pallas_call(mine_kernel, out_shape=(pltpu.VMEM((rows, width), BF16), p...]
    unnamed x32 -> x24, local copies, waits for them, and re-layouts: 1.36 us -> 0.08 us
    all_to_all x1, blocking collectives: 21 us -> 20 us  [body(): lax.all_to_all(partial.reshape(shares, share, width), 'gather', 0, 0, til...]
  transfers between devices with their start and end apart: 5 -> 7, of which waited for: 5 -> 3; matrix products, arithmetic and copies ran while one was open for 1% -> 0% of each run, Pallas kernels for 0% -> 3%
where the time goes in v4:
time: 85.2 us; the launch traced here: 85 us
  blocking collectives  39.6 us (46%)
  starting transfers between devices  28.5 us (33%)
  Pallas kernels  11.9 us (14%)
  waiting for transfers between devices  4.48 us (5%)
    ppermute x6, starting transfers between devices, shifted(): lax.ppermute(block, axis, [(i, (i + step) % count) for i in range(count)])  21.1 us
    all_to_all x1, blocking collectives, body(): lax.all_to_all(partial.reshape(shares, share, width), 'gather', 0, 0, til...  20 us
    all_gather x1, blocking collectives, body(): lax.all_gather(jnp.concatenate([pooled, side], axis=0), 'gather', axis=0,...  17.8 us
    ppermute x1, starting transfers between devices, alternating(): lax.ppermute(block, ('section', 'gather'), [(s * shares + g, (s + 1 - 2 *...  7.42 us
    pallas_call x1, Pallas kernels, body(): pl.pallas_call(coarse_kernel, out_shape=jax.ShapeDtypeStruct((rows, width...  4.44 us
    pallas_call x1, Pallas kernels, body(): pl.pallas_call(fine_kernel, out_shape=(pltpu.VMEM((rows, width), BF16), p...  3.51 us
    ppermute x6, waiting for transfers between devices, shifted(): lax.ppermute(block, axis, [(i, (i + step) % count) for i in range(count)])  3.48 us
    all_gather x1, blocking collectives, across_chip(): lax.all_gather(block, 'gather', axis=0, tiled=True, axis_index_groups=pairs)  1.83 us
  transfers between devices with their start and end apart: 7, of which 3 were waited for; matrix products, arithmetic and copies ran while one was open for 0% of the time, Pallas kernels for 3%

profile of v4, /device:TPU:1, one launch (start us, length us, event | category | flops | bytes accessed | tf_op | source)
XLA Modules:
  0.0 85.0 jit_solution(2116109829550878195)
XLA Ops:
  0.0 1.1 %listed.1.own = bf16[272,512]{1,0:T(8,128)(2,1)S(1)} custom-call(bf16[256,512]{1,0:T(8,128)(2,1)} %features.1, s32[1,8]{1,0:T(1,128)} %bitcast.10), custom_call_target="tpu_custom_call" | custom-call | tf_op jit(solution)/shard_map/listed/pallas_call | solution.py:217
  1.1 4.0 %collective-permute-start = (bf16[272,512]{1,0:T(8,128)(2,1)S(1)}, bf16[272,512]{1,0:T(8,128)(2,1)S(1)}, u32[]{:S(2)}, u32[]{:S(2)}) collective-permute-start(bf16[272,512]{1,0:T(8,128)(2,1)S(1)} %listed.1.own), channel_id=1, source_target_pairs={{0,16},{16,32},{32,48},{48,64},{64,80},{80,96},{96,112},{112,128},... | collective-permute-start | bytes 835592 | tf_op jit(solution)/shard_map/ppermute | solution.py:20
  5.1 6.0 %collective-permute-start.1 = (bf16[272,512]{1,0:T(8,128)(2,1)S(1)}, bf16[272,512]{1,0:T(8,128)(2,1)S(1)}, u32[]{:S(2)}, u32[]{:S(2)}) collective-permute-start(bf16[272,512]{1,0:T(8,128)(2,1)S(1)} %listed.1.own), channel_id=1, source_target_pairs={{0,496},{16,0},{32,16},{48,32},{64,48},{80,64},{96,80},{112,96},{1... | collective-permute-start | bytes 835592 | tf_op jit(solution)/shard_map/ppermute | solution.py:20
  11.1 2.0 %collective-permute-done.before = bf16[272,512]{1,0:T(8,128)(2,1)S(1)} collective-permute-done((bf16[272,512]{1,0:T(8,128)(2,1)S(1)}, bf16[272,512]{1,0:T(8,128)(2,1)S(1)}, u32[]{:S(2)}, u32[]{:S(2)}) %collective-permute-start) | collective-permute-done | bytes 278560 | tf_op jit(solution)/shard_map/ppermute | solution.py:20
  13.1 1.5 %collective-permute-done.1.after = bf16[272,512]{1,0:T(8,128)(2,1)S(1)} collective-permute-done((bf16[272,512]{1,0:T(8,128)(2,1)S(1)}, bf16[272,512]{1,0:T(8,128)(2,1)S(1)}, u32[]{:S(2)}, u32[]{:S(2)}) %collective-permute-start.1) | collective-permute-done | bytes 278560 | tf_op jit(solution)/shard_map/ppermute | solution.py:20
  14.6 0.1 bundle.1
  14.7 5.4 %collective-permute-start.4 = (bf16[256,512]{1,0:T(8,128)(2,1)S(1)}, bf16[256,512]{1,0:T(8,128)(2,1)S(1)}, u32[]{:S(2)}, u32[]{:S(2)}) collective-permute-start(bf16[256,512]{1,0:T(8,128)(2,1)S(1)} %get-tuple-element.24), channel_id=1, source_target_pairs={{0,1},{1,2},{2,3},{3,4},{4,5},{5,6},{6,7},{7,8},{8,9},{9,10},{10,1... | collective-permute-start | bytes 786440 | tf_op jit(solution)/shard_map/ppermute | solution.py:20
  20.1 1.2 %collective-permute-start.5 = (bf16[256,512]{1,0:T(8,128)(2,1)S(1)}, bf16[256,512]{1,0:T(8,128)(2,1)S(1)}, u32[]{:S(2)}, u32[]{:S(2)}) collective-permute-start(bf16[256,512]{1,0:T(8,128)(2,1)S(1)} %get-tuple-element.25), channel_id=1, source_target_pairs={{0,15},{1,0},{2,1},{3,2},{4,3},{5,4},{6,5},{7,6},{8,7},{9,8},{10,9... | collective-permute-start | bytes 786440 | tf_op jit(solution)/shard_map/ppermute | solution.py:20
  21.3 0.0 copy-start.4
  21.3 0.0 copy-start.5
  21.3 0.0 copy-start.6
  21.4 0.0 copy-start.9
  21.4 0.0 copy-start.10
  21.4 0.5 collective-permute-start.2
  21.9 4.0 %collective-permute-start.3 = (bf16[128,512]{1,0:T(8,128)(2,1)S(1)}, bf16[128,512]{1,0:T(8,128)(2,1)S(1)}, u32[]{:S(2)}, u32[]{:S(2)}) collective-permute-start(bf16[128,512]{1,0:T(8,128)(2,1)S(1)} %get-tuple-element.23), channel_id=1, source_target_pairs={{0,15},{1,0},{2,1},{3,2},{4,3},{5,4},{6,5},{7,6},{8,7},{9,8},{10,9... | collective-permute-start | bytes 393224 | tf_op jit(solution)/shard_map/ppermute | solution.py:20
  25.9 1.7 %mine.1 = (bf16[256,512]{1,0:T(8,128)(2,1)S(1)}, f32[256,512]{1,0:T(8,128)S(1)}, bf16[512,512]{1,0:T(8,128)(2,1)S(1)}, s32[256,6]{1,0:T(8,128)S(1)}, s32[256,6]{1,0:T(8,128)S(1)}) custom-call(bf16[272,512]{1,0:T(8,128)(2,1)S(1)} %listed.1.own, s32[6,256]{1,0:T(8,128)} %ids.2, bf16[512,512]{1,0:T(8,128)(2,1)} %dst.2, bf16[512,512]{1,0:T(8,128)(2,1)} %src.2, ...), custom_call_target="tpu_custom_call" | custom-call | tf_op jit(solution)/shard_map/mine/pallas_call | solution.py:241
  27.5 1.1 %early.1.base = f32[1536,512]{1,0:T(8,128)S(1)} custom-call(bf16[256,512]{1,0:T(8,128)(2,1)S(1)} %get-tuple-element.17.own_sources, f32[256,512]{1,0:T(8,128)S(1)} %get-tuple-element.18.target_half, bf16[256,512]{1,0:T(8,128)(2,1)S(1)} %get-tuple-element.19.beside, s32[256,6]{1,0:T(8,128)S(1)} %get-tuple-element.20.place, ...), custom_call_target="tpu_custom_call" | custom-call | tf_op jit(solution)/shard_map/early/pallas_call | solution.py:253
  28.7 0.0 collective-permute-done.2.below_own
  28.7 0.0 collective-permute-done.3.above_own
  28.7 0.0 collective-permute-done.4.below
  28.7 0.0 collective-permute-done.5.above
  28.7 0.0 copy-done.4
  28.7 0.0 copy-done.5
  28.7 0.0 copy-done.6
  28.8 0.0 copy-done.9
  28.8 0.0 copy-done.10
  28.8 0.0 copy-start
  28.8 0.0 copy-start.1
  28.8 0.0 copy-start.2
  28.8 0.0 copy-start.3
  28.8 0.0 copy-start.7
  28.8 0.0 copy-start.8
  28.9 0.0 copy-start.11
  28.9 3.5 %fine.1 = (bf16[256,512]{1,0:T(8,128)(2,1)S(1)}, bf16[256,512]{1,0:T(8,128)(2,1)S(1)}) custom-call(bf16[272,512]{1,0:T(8,128)(2,1)S(1)} %listed.1.own, f32[1536,512]{1,0:T(8,128)S(1)} %early.1.base, bf16[128,512]{1,0:T(8,128)(2,1)S(1)} %collective-permute-done.2.below_own, bf16[128,512]{1,0:T(8,128)(2,1)S(1)} %collective-permute-done.3.above_own, ...), custom_call_target="tpu_custom_call" | custom-call | tf_op jit(solution)/shard_map/fine/pallas_call | solution.py:260
  32.4 20.0 %all_to_all.5 = bf16[16,16,512]{2,1,0:T(8,128)(2,1)S(1)} all-to-all(bf16[16,16,512]{2,1,0:T(8,128)(2,1)S(1)} %bitcast.5), channel_id=1, replica_groups=mesh['section'=32,'gather'=16] {'gather'}, dimensions={0} | all-to-all | bytes 524288 | tf_op jit(solution)/shard_map/all_to_all | solution.py:273
  52.4 1.8 %all_gather.6 = bf16[32,512]{1,0:T(8,128)(2,1)S(1)} all-gather(bf16[16,512]{1,0:T(8,128)(2,1)S(1)} %multiply_convert_fusion), channel_id=1, replica_groups={{0,1},{2,3},{4,5},{6,7},{8,9},{10,11},{12,13},{14,15},{16,17},{18,19},{..., dimensions={0}, use_global_device_ids=true | all-gather | bytes 49152 | tf_op jit(solution)/shard_map/all_gather | solution.py:38
  54.3 7.4 %collective-permute-start.6 = (bf16[32,512]{1,0:T(8,128)(2,1)S(1)}, bf16[32,512]{1,0:T(8,128)(2,1)S(1)}, u32[]{:S(2)}, u32[]{:S(2)}) collective-permute-start(bf16[32,512]{1,0:T(8,128)(2,1)S(1)} %all_gather.6), channel_id=1, source_target_pairs={{0,16},{1,497},{2,18},{3,499},{4,20},{5,501},{6,22},{7,503},{8,24}... | collective-permute-start | bytes 98312 | tf_op jit(solution)/shard_map/ppermute | solution.py:25
  61.7 1.0 %collective-permute-done.6 = bf16[32,512]{1,0:T(8,128)(2,1)S(1)} collective-permute-done((bf16[32,512]{1,0:T(8,128)(2,1)S(1)}, bf16[32,512]{1,0:T(8,128)(2,1)S(1)}, u32[]{:S(2)}, u32[]{:S(2)}) %collective-permute-start.6) | collective-permute-done | bytes 32800 | tf_op jit(solution)/shard_map/ppermute | solution.py:25
  62.7 17.8 %all_gather.7.spread = bf16[768,512]{1,0:T(8,128)(2,1)S(1)} all-gather(bf16[48,512]{1,0:T(8,128)(2,1)S(1)} %pad_maximum_fusion), channel_id=1, replica_groups=mesh['section'=32,'gather'=16] {'gather'}, dimensions={0}, use_global_device_ids=true | all-gather | bytes 835584 | tf_op jit(solution)/shard_map/all_gather | solution.py:276
  80.5 0.0 copy-done
  80.5 0.0 copy-done.1
  80.5 0.0 copy-done.2
  80.5 0.0 copy-done.3
  80.5 0.0 copy-done.7
  80.5 0.0 copy-done.8
  80.5 0.0 copy-done.11
  80.5 4.4 %coarse.1 = bf16[256,512]{1,0:T(8,128)(2,1)} custom-call(bf16[768,512]{1,0:T(8,128)(2,1)S(1)} %all_gather.7.spread, bf16[256,512]{1,0:T(8,128)(2,1)S(1)} %get-tuple-element.28.fine_rows, s32[6,256]{1,0:T(8,128)S(1)} %copy-done.7, s32[1,256]{1,0:T(1,128)S(1)} %bitcast.7, bf16[512,512]{1,0:T(8,128)(2,1)S(1)} %copy-done, bf16[512,512]{1,0:T(8,128)(2,1)S(1)} %copy-done.1, ...), custom_call_target="tpu_custom_call" | custom-call | tf_op jit(solution)/shard_map/coarse/pallas_call | solution.py:278
  (4 shorter events, 0.1 us)
Async XLA Ops:
  1.1 12.0 %collective-permute-start = (bf16[272,512]{1,0:T(8,128)(2,1)S(1)}, bf16[272,512]{1,0:T(8,128)(2,1)S(1)}, u32[]{:S(2)}, u32[]{:S(2)}) collective-permute-start(bf16[272,512]{1,0:T(8,128)(2,1)S(1)} %listed.1.own), channel_id=1, source_target_pairs={{0,16},{16,32},{32,48},{48,64},{64,80},{80,96},{96,112},{112,128},... | collective-permute-start | bytes 835592 | tf_op jit(solution)/shard_map/ppermute | solution.py:20
  5.1 9.5 %collective-permute-start.1 = (bf16[272,512]{1,0:T(8,128)(2,1)S(1)}, bf16[272,512]{1,0:T(8,128)(2,1)S(1)}, u32[]{:S(2)}, u32[]{:S(2)}) collective-permute-start(bf16[272,512]{1,0:T(8,128)(2,1)S(1)} %listed.1.own), channel_id=1, source_target_pairs={{0,496},{16,0},{32,16},{48,32},{64,48},{80,64},{96,80},{112,96},{1... | collective-permute-start | bytes 835592 | tf_op jit(solution)/shard_map/ppermute | solution.py:20
  14.7 14.0 %collective-permute-start.4 = (bf16[256,512]{1,0:T(8,128)(2,1)S(1)}, bf16[256,512]{1,0:T(8,128)(2,1)S(1)}, u32[]{:S(2)}, u32[]{:S(2)}) collective-permute-start(bf16[256,512]{1,0:T(8,128)(2,1)S(1)} %get-tuple-element.24), channel_id=1, source_target_pairs={{0,1},{1,2},{2,3},{3,4},{4,5},{5,6},{6,7},{7,8},{8,9},{9,10},{10,1... | collective-permute-start | bytes 786440 | tf_op jit(solution)/shard_map/ppermute | solution.py:20
  20.1 8.7 %collective-permute-start.5 = (bf16[256,512]{1,0:T(8,128)(2,1)S(1)}, bf16[256,512]{1,0:T(8,128)(2,1)S(1)}, u32[]{:S(2)}, u32[]{:S(2)}) collective-permute-start(bf16[256,512]{1,0:T(8,128)(2,1)S(1)} %get-tuple-element.25), channel_id=1, source_target_pairs={{0,15},{1,0},{2,1},{3,2},{4,3},{5,4},{6,5},{7,6},{8,7},{9,8},{10,9... | collective-permute-start | bytes 786440 | tf_op jit(solution)/shard_map/ppermute | solution.py:20
  21.3 7.4 %copy-start.4 = (bf16[512,512]{1,0:T(8,128)(2,1)S(1)}, bf16[512,512]{1,0:T(8,128)(2,1)}, u32[]{:S(2)}) copy-start(bf16[512,512]{1,0:T(8,128)(2,1)} %edge.2) | copy-start | bytes 1572868
  21.3 7.4 %copy-start.5 = (bf16[512,512]{1,0:T(8,128)(2,1)S(1)}, bf16[512,512]{1,0:T(8,128)(2,1)}, u32[]{:S(2)}) copy-start(bf16[512,512]{1,0:T(8,128)(2,1)} %node.2) | copy-start | bytes 1572868
  21.3 7.4 %copy-start.6 = (f32[2,512]{1,0:T(2,128)S(1)}, f32[2,512]{1,0:T(2,128)}, u32[]{:S(2)}) copy-start(f32[2,512]{1,0:T(2,128)} %bias.4) | copy-start | bytes 12292
  21.4 7.4 %copy-start.9 = (s32[256]{0:T(256)S(1)}, s32[256]{0:T(256)}, u32[]{:S(2)}) copy-start(s32[256]{0:T(256)} %param.20) | copy-start | bytes 3076
  21.4 7.4 %copy-start.10 = (f32[512]{0:T(512)S(1)}, f32[512]{0:T(512)}, u32[]{:S(2)}) copy-start(f32[512]{0:T(512)} %param.27) | copy-start | bytes 6148
  21.4 7.3 %collective-permute-start.2 = (bf16[128,512]{1,0:T(8,128)(2,1)S(1)}, bf16[128,512]{1,0:T(8,128)(2,1)S(1)}, u32[]{:S(2)}, u32[]{:S(2)}) collective-permute-start(bf16[128,512]{1,0:T(8,128)(2,1)S(1)} %get-tuple-element.22), channel_id=1, source_target_pairs={{0,1},{1,2},{2,3},{3,4},{4,5},{5,6},{6,7},{7,8},{8,9},{9,10},{10,1... | collective-permute-start | bytes 393224 | tf_op jit(solution)/shard_map/ppermute | solution.py:20
  21.9 6.8 %collective-permute-start.3 = (bf16[128,512]{1,0:T(8,128)(2,1)S(1)}, bf16[128,512]{1,0:T(8,128)(2,1)S(1)}, u32[]{:S(2)}, u32[]{:S(2)}) collective-permute-start(bf16[128,512]{1,0:T(8,128)(2,1)S(1)} %get-tuple-element.23), channel_id=1, source_target_pairs={{0,15},{1,0},{2,1},{3,2},{4,3},{5,4},{6,5},{7,6},{8,7},{9,8},{10,9... | collective-permute-start | bytes 393224 | tf_op jit(solution)/shard_map/ppermute | solution.py:20
  28.8 51.7 %copy-start = (bf16[512,512]{1,0:T(8,128)(2,1)S(1)}, bf16[512,512]{1,0:T(8,128)(2,1)}, u32[]{:S(2)}) copy-start(bf16[512,512]{1,0:T(8,128)(2,1)} %dst.3) | copy-start | bytes 1572868
  28.8 51.7 %copy-start.1 = (bf16[512,512]{1,0:T(8,128)(2,1)S(1)}, bf16[512,512]{1,0:T(8,128)(2,1)}, u32[]{:S(2)}) copy-start(bf16[512,512]{1,0:T(8,128)(2,1)} %src.3) | copy-start | bytes 1572868
  28.8 51.7 %copy-start.2 = (bf16[512,512]{1,0:T(8,128)(2,1)S(1)}, bf16[512,512]{1,0:T(8,128)(2,1)}, u32[]{:S(2)}) copy-start(bf16[512,512]{1,0:T(8,128)(2,1)} %edge.3) | copy-start | bytes 1572868
  28.8 51.7 %copy-start.3 = (bf16[512,512]{1,0:T(8,128)(2,1)S(1)}, bf16[512,512]{1,0:T(8,128)(2,1)}, u32[]{:S(2)}) copy-start(bf16[512,512]{1,0:T(8,128)(2,1)} %node.3) | copy-start | bytes 1572868
  28.8 51.7 %copy-start.7 = (s32[6,256]{1,0:T(8,128)S(1)}, s32[6,256]{1,0:T(8,128)}, u32[]{:S(2)}) copy-start(s32[6,256]{1,0:T(8,128)} %ids.3) | copy-start | bytes 18436
  28.8 51.7 %copy-start.8 = (f32[2,512]{1,0:T(2,128)S(1)}, f32[2,512]{1,0:T(2,128)}, u32[]{:S(2)}) copy-start(f32[2,512]{1,0:T(2,128)} %bias.5) | copy-start | bytes 12292
  28.9 51.6 %copy-start.11 = (f32[512]{0:T(512)S(1)}, f32[512]{0:T(512)}, u32[]{:S(2)}) copy-start(f32[512]{0:T(512)} %param.33) | copy-start | bytes 6148
  54.3 8.4 %collective-permute-start.6 = (bf16[32,512]{1,0:T(8,128)(2,1)S(1)}, bf16[32,512]{1,0:T(8,128)(2,1)S(1)}, u32[]{:S(2)}, u32[]{:S(2)}) collective-permute-start(bf16[32,512]{1,0:T(8,128)(2,1)S(1)} %all_gather.6), channel_id=1, source_target_pairs={{0,16},{1,497},{2,18},{3,499},{4,20},{5,501},{6,22},{7,503},{8,24}... | collective-permute-start | bytes 98312 | tf_op jit(solution)/shard_map/ppermute | solution.py:25
